TPU v7x, 256 devices: a whole 4x4x8 slice. The times are simulated.
256 devices in a mesh: row: 16 (over z_hi, x), col: 16 (over y, z_lo, core).
Axes of the slice: x: 4, y: 4, z: 8 (z_hi: 4, z_lo: 2; z = z_hi * 2 + z_lo), core: 2. Of those that a mesh axis runs over, the one named last changes fastest.
Arguments:
- start_vectors: float32 [64, 32768], P(None, ('row', 'col')), may hold values from -6 to 6
- scaling: float32 [32768], P(('row', 'col')), may hold values from 0.25 to 1.75
- block_values: bfloat16 [16, 16, 128, 128, 128], P('row', 'col'), may hold values from -0.046875 to 0.046875
- block_places: int32 [16, 16, 2, 128], P('row', 'col'), may hold values from 0 to 15, as said below
- block_counts: int32 [16, 16], P('row', 'col'), may hold values from 16 to 128, as said below
Outputs:
- filtered: float32 [64, 32768], P(None, ('row', 'col'))
Inputs may be any that keep to these rules, and one draw needn't show every extreme that they name: `block_places`: within each device's 128 slots the positions (block row, block column) are distinct; entry 0 is the local block row (below 16), entry 1 the local block column (below 16). Slots at or after the device's count are not part of the matrix. `block_counts`: some device has all 128 slots live.
All inputs are finite; a program needn't handle non-finite values.
Results may differ from a plain program's by a relative error of at most 0.0038.
Values may be sent and summed in bfloat16 or wider, within the bound.
A program may use at most 128 MiB of HBM per device.

v0:
```python
import jax
import jax.numpy as jnp
from jax import lax
from jax.sharding import PartitionSpec as P

STEPS = 3


center_shift = 0.5
half_width = 3.0


def laid_out(blocks, dim):
    blocks = jnp.moveaxis(blocks, 0, dim)
    shape = blocks.shape
    return blocks.reshape(*shape[:dim], shape[dim] * shape[dim + 1], *shape[dim + 2 :])


def sent_to_all(value, axis):
    copies = jnp.broadcast_to(value, (lax.axis_size(axis), *value.shape))
    return lax.all_to_all(copies, axis, split_axis=0, concat_axis=0, tiled=True)


def collect(value, axis, dim):
    return laid_out(sent_to_all(value, axis), dim)


def in_blocks(value, dim, devices):
    before, after = (value.shape[:dim], value.shape[dim + 1 :])
    return jnp.moveaxis(value.reshape(*before, devices, -1, *after), dim, 0)


def summed_on_arrival(value, axis, dim):
    blocks = in_blocks(value, dim, lax.axis_size(axis))
    arrived = lax.all_to_all(blocks, axis, split_axis=0, concat_axis=0, tiled=True)
    return arrived.sum(axis=0)


def build_tile(slabs, row_places, col_places, live_count, row_blocks, col_blocks):
    block_len = slabs.shape[-1]
    live_mask = jnp.arange(slabs.shape[0]) < live_count
    masked = jnp.where(live_mask[:, None, None], slabs, jnp.zeros_like(slabs))
    empty = jnp.zeros((row_blocks, col_blocks, block_len, block_len), jnp.bfloat16)
    placed = empty.at[row_places, col_places].add(masked)
    return placed.transpose(0, 2, 1, 3).reshape(row_blocks * block_len, col_blocks * block_len)


def per_device(start_vectors, scaling, block_values, block_places, block_counts):
    row_size = lax.axis_size("row")
    col_size = lax.axis_size("col")
    tile_ratio = row_size // col_size
    piece_len = start_vectors.shape[1]
    vec_count = start_vectors.shape[0]
    tile_len = piece_len * col_size
    slot_count = block_values.shape[2]
    block_len = block_values.shape[-1]
    row_blocks = tile_len // block_len
    col_blocks = row_blocks * tile_ratio
    slabs = block_values.reshape(slot_count, block_len, block_len)
    places = block_places.reshape(2, slot_count)
    row_places = places[0]
    col_places = places[1]
    live_count = block_counts.reshape(())
    tile = build_tile(slabs, row_places, col_places, live_count, row_blocks, col_blocks)
    current = start_vectors
    previous = current
    for iterate in range(STEPS):
        scaled_now = (scaling[None, :] * current).astype(jnp.bfloat16)
        v_rows = collect(scaled_now, "col", 1)
        grid_column = collect(scaled_now, "row", 1)
        grid_column = grid_column.reshape(vec_count, col_size, tile_ratio, piece_len)
        v_cols = lax.all_to_all(grid_column, "col", split_axis=1, concat_axis=3, tiled=True)
        v_cols = v_cols.reshape(vec_count, tile_ratio * tile_len)
        direct = lax.dot_general(
            v_cols, tile, (((1,), (1,)), ((), ())), preferred_element_type=jnp.float32
        )
        transposed = jnp.dot(v_rows, tile, preferred_element_type=jnp.float32)
        spread = transposed.reshape(vec_count, tile_ratio, col_size, piece_len)
        owned = lax.all_to_all(spread, "col", split_axis=2, concat_axis=1, tiled=True)
        transposed_own = summed_on_arrival(owned, "row", 1).reshape(vec_count, piece_len)
        applied = summed_on_arrival(direct, "col", 1) + transposed_own
        mapped = scaling[None, :] * applied - center_shift * current
        if iterate == 0:
            updated = mapped / half_width
        else:
            updated = 2.0 / half_width * mapped - previous
        previous = current
        current = updated
    return current


def solution(mesh):
    in_specs = (
        P(None, ("row", "col")),
        P(("row", "col")),
        P("row", "col", None, None, None),
        P("row", "col", None, None),
        P("row", "col"),
    )
    out_specs = P(None, ("row", "col"))
    return jax.shard_map(
        per_device, mesh=mesh, in_specs=in_specs, out_specs=out_specs, check_vma=False
    )
```

profile of v0, /device:TPU:8, one launch (start us, length us, event | category | flops | bytes accessed | tf_op | source)
XLA Modules:
  0.0 355.7 jit_solution(15794602470778312536)
XLA Ops:
  1.5 6.3 %all-to-all-start.3 = ((bf16[16,64,128]{2,1,0:T(8,128)(2,1)}), bf16[16,64,128]{2,1,0:T(8,128)(2,1)S(1)}, u32[]{:S(2)}, u32[]{:S(2)}) async-start(bf16[16,64,128]{2,1,0:T(8,128)(2,1)} %broadcast_in_dim.18), calls=%async_computation.3 | async-start | bytes 524288 | tf_op jit(solution)/shard_map/all_to_all | solution.py:21
  13.3 10.2 %all-to-all-start = ((bf16[16,64,128]{2,1,0:T(8,128)(2,1)}), bf16[16,64,128]{2,1,0:T(8,128)(2,1)}, u32[]{:S(2)}, u32[]{:S(2)}) async-start(bf16[16,64,128]{2,1,0:T(8,128)(2,1)} %broadcast_in_dim.18), calls=%async_computation | async-start | bytes 524288 | tf_op jit(solution)/shard_map/all_to_all | solution.py:21
  28.0 5.4 %broadcast_in_dim.19 = bf16[16,16,128,128]{3,2,1,0:T(8,128)(2,1)} broadcast(bf16[]{:T(256)} %constant.2.clone.1), dimensions={} | broadcast | bytes 8388610 | tf_op jit(solution)/shard_map/broadcast_in_dim | solution.py:43
  33.3 27.0 %scatter_fusion = bf16[16,16,128,128]{3,2,1,0:T(8,128)(2,1)} fusion(bf16[16,16,128,128]{3,2,1,0:T(8,128)(2,1)} %broadcast_in_dim.19, s32[128]{0:T(128)S(1)} %fusion.1, bf16[128,128,128]{2,1,0:T(8,128)(2,1)} %bitcast_select_fusion), kind=kCustom, calls=%fused_computation | custom fusion | flops 2097152 | bytes 12583936 | tf_op jit(solution)/shard_map/scatter-add | solution.py:44
  60.3 13.7 %copy.20 = bf16[16,128,16,128]{3,2,1,0:T(8,128)(2,1)} copy(bf16[16,128,16,128]{3,1,2,0:T(8,128)(2,1)} %bitcast.106) | data formatting | bytes 16777216 | tf_op jit(solution)/shard_map/transpose | solution.py:45
  74.0 10.9 %copy.44 = bf16[256,8,16,128]{3,1,2,0:T(8,128)(2,1)} copy(bf16[256,8,16,128]{3,2,1,0:T(8,128)(2,1)} %bitcast.109) | data formatting | bytes 16777216
  84.9 12.4 %copy.41 = bf16[2048,2048]{1,0:T(8,128)(2,1)} copy(bf16[2048,2048]{0,1:T(8,128)(2,1)} %bitcast.108) | data formatting | bytes 16777216 | tf_op jit(solution)/shard_map/reshape.59
  97.6 6.1 %all-to-all-start.1 = ((bf16[64,16,1,128]{3,0,2,1:T(8,128)(2,1)}), bf16[64,16,1,128]{3,0,2,1:T(8,128)(2,1)S(1)}, u32[]{:S(2)}, u32[]{:S(2)}) async-start(bf16[64,16,1,128]{3,0,2,1:T(8,128)(2,1)} %bitcast.2), calls=%async_computation.1 | async-start | bytes 524288 | tf_op jit(solution)/shard_map/all_to_all | solution.py:72
  103.6 6.9 %convolution_bitcast_fusion.4 = f32[64,1,16,128]{3,0,1,2:T(8,128)} fusion(bf16[64,2048,1]{1,0,2:T(8,128)(2,1)S(1)} %reshape.181, bf16[16,128,2048]{2,1,0:T(8,128)(2,1)} %bitcast.100), kind=kOutput, calls=%fused_computation.7 | convolution fusion | flops 536870912 | bytes 9175040 | tf_op jit(solution)/shard_map/dot_general | solution.py:77
  110.5 5.8 %all-to-all-start.4 = ((f32[64,1,16,128]{3,0,1,2:T(8,128)}), f32[64,1,16,128]{3,0,1,2:T(8,128)}, u32[]{:S(2)}, u32[]{:S(2)}) async-start(f32[64,1,16,128]{3,0,1,2:T(8,128)} %convolution_bitcast_fusion.4), calls=%async_computation.4 | async-start | bytes 1048576 | tf_op jit(solution)/shard_map/all_to_all | solution.py:79
  116.3 12.3 %copy.17 = bf16[16,128,16,128]{1,3,2,0:T(8,128)(2,1)} copy(bf16[16,128,16,128]{3,1,2,0:T(8,128)(2,1)} %bitcast.107) | data formatting | bytes 16777216 | tf_op jit(solution)/shard_map/transpose | solution.py:45
  128.9 4.9 %convolution_bitcast_fusion.5 = f32[16,64,128]{2,1,0:T(8,128)S(1)} fusion(bf16[64,2048,1]{1,0,2:T(8,128)(2,1)S(1)} %reshape.180, bf16[16,128,2048]{1,2,0:T(8,128)(2,1)} %bitcast.103), kind=kOutput, calls=%fused_computation.8 | convolution fusion | flops 536870912 | bytes 9175040 | tf_op jit(solution)/shard_map/dot_general | solution.py:74
  133.8 13.8 %all_to_all.114 = f32[16,64,128]{2,1,0:T(8,128)S(1)} all-to-all(f32[16,64,128]{2,1,0:T(8,128)S(1)} %convolution_bitcast_fusion.5), channel_id=1, replica_groups=mesh['row'=16,'col'=16] {'col'}, dimensions={0} | all-to-all | bytes 1048576 | tf_op jit(solution)/shard_map/all_to_all | solution.py:35
  147.6 9.6 %all-to-all-start.5 = ((f32[16,64,1,1,128]{4,1,3,2,0:T(8,128)}), f32[16,64,1,1,128]{4,1,3,2,0:T(8,128)S(1)}, u32[]{:S(2)}, u32[]{:S(2)}) async-start(f32[16,64,1,1,128]{4,1,3,2,0:T(8,128)} %bitcast.17), calls=%async_computation.5 | async-start | bytes 1048576 | tf_op jit(solution)/shard_map/all_to_all | solution.py:35
  157.3 16.8 %all-to-all-done.5 = f32[16,64,1,1,128]{4,1,3,2,0:T(8,128)S(1)} async-done(((f32[16,64,1,1,128]{4,1,3,2,0:T(8,128)}), f32[16,64,1,1,128]{4,1,3,2,0:T(8,128)S(1)}, u32[]{:S(2)}, u32[]{:S(2)}) %all-to-all-start.5) | async-done | bytes 524320 | tf_op jit(solution)/shard_map/all_to_all | solution.py:35
  174.8 12.0 %all_to_all.115 = bf16[16,64,128]{2,1,0:T(8,128)(2,1)S(1)} all-to-all(bf16[16,64,128]{2,1,0:T(8,128)(2,1)} %broadcast_in_dim.22), channel_id=1, replica_groups=mesh['row'=16,'col'=16] {'col'}, dimensions={0} | all-to-all | bytes 524288 | tf_op jit(solution)/shard_map/all_to_all | solution.py:21
  191.7 13.0 %all-to-all-done.6 = bf16[16,64,128]{2,1,0:T(8,128)(2,1)} async-done(((bf16[16,64,128]{2,1,0:T(8,128)(2,1)}), bf16[16,64,128]{2,1,0:T(8,128)(2,1)}, u32[]{:S(2)}, u32[]{:S(2)}) %all-to-all-start.6) | async-done | bytes 262176 | tf_op jit(solution)/shard_map/all_to_all | solution.py:21
  204.7 5.1 %all-to-all-start.7 = ((bf16[64,16,1,128]{3,0,2,1:T(8,128)(2,1)}), bf16[64,16,1,128]{3,0,2,1:T(8,128)(2,1)S(1)}, u32[]{:S(2)}, u32[]{:S(2)}) async-start(bf16[64,16,1,128]{3,0,2,1:T(8,128)(2,1)} %bitcast.20), calls=%async_computation.7 | async-start | bytes 524288 | tf_op jit(solution)/shard_map/all_to_all | solution.py:72
  209.8 6.8 %convolution_bitcast_fusion.2 = f32[64,1,16,128]{3,0,1,2:T(8,128)} fusion(bf16[64,2048,1]{1,0,2:T(8,128)(2,1)S(1)} %reshape.183, bf16[16,128,2048]{2,1,0:T(8,128)(2,1)} %bitcast.101), kind=kOutput, calls=%fused_computation.5 | convolution fusion | flops 536870912 | bytes 9175040 | tf_op jit(solution)/shard_map/dot_general | solution.py:77
  216.6 5.8 %all-to-all-start.10 = ((f32[64,1,16,128]{3,0,1,2:T(8,128)}), f32[64,1,16,128]{3,0,1,2:T(8,128)}, u32[]{:S(2)}, u32[]{:S(2)}) async-start(f32[64,1,16,128]{3,0,1,2:T(8,128)} %convolution_bitcast_fusion.2), calls=%async_computation.10 | async-start | bytes 1048576 | tf_op jit(solution)/shard_map/all_to_all | solution.py:79
  222.7 4.9 %convolution_bitcast_fusion.3 = f32[16,64,128]{2,1,0:T(8,128)S(1)} fusion(bf16[64,2048,1]{1,0,2:T(8,128)(2,1)S(1)} %reshape.182, bf16[16,128,2048]{1,2,0:T(8,128)(2,1)} %bitcast.104), kind=kOutput, calls=%fused_computation.6 | convolution fusion | flops 536870912 | bytes 9175040 | tf_op jit(solution)/shard_map/dot_general | solution.py:74
  230.8 13.4 %all_to_all.116 = f32[16,64,128]{2,1,0:T(8,128)S(1)} all-to-all(f32[16,64,128]{2,1,0:T(8,128)S(1)} %convolution_bitcast_fusion.3), channel_id=1, replica_groups=mesh['row'=16,'col'=16] {'col'}, dimensions={0} | all-to-all | bytes 1048576 | tf_op jit(solution)/shard_map/all_to_all | solution.py:35
  248.1 16.0 %all-to-all-done.11 = f32[16,64,1,1,128]{4,1,3,2,0:T(8,128)S(1)} async-done(((f32[16,64,1,1,128]{4,1,3,2,0:T(8,128)}), f32[16,64,1,1,128]{4,1,3,2,0:T(8,128)S(1)}, u32[]{:S(2)}, u32[]{:S(2)}) %all-to-all-start.11) | async-done | bytes 524320 | tf_op jit(solution)/shard_map/all_to_all | solution.py:35
  264.9 12.8 %all_to_all.117 = bf16[16,64,128]{2,1,0:T(8,128)(2,1)S(1)} all-to-all(bf16[16,64,128]{2,1,0:T(8,128)(2,1)} %broadcast_in_dim.40), channel_id=1, replica_groups=mesh['row'=16,'col'=16] {'col'}, dimensions={0} | all-to-all | bytes 524288 | tf_op jit(solution)/shard_map/all_to_all | solution.py:21
  277.7 4.6 %all-to-all-start.12 = ((bf16[16,64,128]{2,1,0:T(8,128)(2,1)}), bf16[16,64,128]{2,1,0:T(8,128)(2,1)}, u32[]{:S(2)}, u32[]{:S(2)}) async-start(bf16[16,64,128]{2,1,0:T(8,128)(2,1)} %broadcast_in_dim.40), calls=%async_computation.12 | async-start | bytes 524288 | tf_op jit(solution)/shard_map/all_to_all | solution.py:21
  282.6 13.0 %all-to-all-done.12 = bf16[16,64,128]{2,1,0:T(8,128)(2,1)} async-done(((bf16[16,64,128]{2,1,0:T(8,128)(2,1)}), bf16[16,64,128]{2,1,0:T(8,128)(2,1)}, u32[]{:S(2)}, u32[]{:S(2)}) %all-to-all-start.12) | async-done | bytes 262176 | tf_op jit(solution)/shard_map/all_to_all | solution.py:21
  295.7 5.1 %all-to-all-start.13 = ((bf16[64,16,1,128]{3,0,2,1:T(8,128)(2,1)}), bf16[64,16,1,128]{3,0,2,1:T(8,128)(2,1)S(1)}, u32[]{:S(2)}, u32[]{:S(2)}) async-start(bf16[64,16,1,128]{3,0,2,1:T(8,128)(2,1)} %bitcast.30), calls=%async_computation.13 | async-start | bytes 524288 | tf_op jit(solution)/shard_map/all_to_all | solution.py:72
  300.8 6.8 %convolution_bitcast_fusion = f32[64,1,16,128]{3,0,1,2:T(8,128)} fusion(bf16[64,2048,1]{1,0,2:T(8,128)(2,1)S(1)} %reshape.185, bf16[16,128,2048]{2,1,0:T(8,128)(2,1)} %bitcast.102), kind=kOutput, calls=%fused_computation.3 | convolution fusion | flops 536870912 | bytes 9175040 | tf_op jit(solution)/shard_map/dot_general | solution.py:77
  307.6 5.8 %all-to-all-start.16 = ((f32[64,1,16,128]{3,0,1,2:T(8,128)}), f32[64,1,16,128]{3,0,1,2:T(8,128)}, u32[]{:S(2)}, u32[]{:S(2)}) async-start(f32[64,1,16,128]{3,0,1,2:T(8,128)} %convolution_bitcast_fusion), calls=%async_computation.16 | async-start | bytes 1048576 | tf_op jit(solution)/shard_map/all_to_all | solution.py:79
  313.7 4.9 %convolution_bitcast_fusion.1 = f32[16,64,128]{2,1,0:T(8,128)S(1)} fusion(bf16[64,2048,1]{1,0,2:T(8,128)(2,1)S(1)} %reshape.184, bf16[16,128,2048]{1,2,0:T(8,128)(2,1)} %bitcast.105), kind=kOutput, calls=%fused_computation.4 | convolution fusion | flops 536870912 | bytes 9175040 | tf_op jit(solution)/shard_map/dot_general | solution.py:74
  321.7 13.4 %all_to_all.118 = f32[16,64,128]{2,1,0:T(8,128)S(1)} all-to-all(f32[16,64,128]{2,1,0:T(8,128)S(1)} %convolution_bitcast_fusion.1), channel_id=1, replica_groups=mesh['row'=16,'col'=16] {'col'}, dimensions={0} | all-to-all | bytes 1048576 | tf_op jit(solution)/shard_map/all_to_all | solution.py:35
  339.1 16.0 %all-to-all-done.17 = f32[16,64,1,1,128]{4,1,3,2,0:T(8,128)S(1)} async-done(((f32[16,64,1,1,128]{4,1,3,2,0:T(8,128)}), f32[16,64,1,1,128]{4,1,3,2,0:T(8,128)S(1)}, u32[]{:S(2)}, u32[]{:S(2)}) %all-to-all-start.17) | async-done | bytes 524320 | tf_op jit(solution)/shard_map/all_to_all | solution.py:35
  (44 shorter events, 33.6 us)
Async XLA Ops:
  1.5 11.7 %all-to-all-start.3 = ((bf16[16,64,128]{2,1,0:T(8,128)(2,1)}), bf16[16,64,128]{2,1,0:T(8,128)(2,1)S(1)}, u32[]{:S(2)}, u32[]{:S(2)}) async-start(bf16[16,64,128]{2,1,0:T(8,128)(2,1)} %broadcast_in_dim.18), calls=%async_computation.3 | async-start | bytes 524288 | tf_op jit(solution)/shard_map/all_to_all | solution.py:21
  13.3 84.3 %all-to-all-start = ((bf16[16,64,128]{2,1,0:T(8,128)(2,1)}), bf16[16,64,128]{2,1,0:T(8,128)(2,1)}, u32[]{:S(2)}, u32[]{:S(2)}) async-start(bf16[16,64,128]{2,1,0:T(8,128)(2,1)} %broadcast_in_dim.18), calls=%async_computation | async-start | bytes 524288 | tf_op jit(solution)/shard_map/all_to_all | solution.py:21
  97.6 13.0 %all-to-all-start.1 = ((bf16[64,16,1,128]{3,0,2,1:T(8,128)(2,1)}), bf16[64,16,1,128]{3,0,2,1:T(8,128)(2,1)S(1)}, u32[]{:S(2)}, u32[]{:S(2)}) async-start(bf16[64,16,1,128]{3,0,2,1:T(8,128)(2,1)} %bitcast.2), calls=%async_computation.1 | async-start | bytes 524288 | tf_op jit(solution)/shard_map/all_to_all | solution.py:72
  110.5 23.3 %all-to-all-start.4 = ((f32[64,1,16,128]{3,0,1,2:T(8,128)}), f32[64,1,16,128]{3,0,1,2:T(8,128)}, u32[]{:S(2)}, u32[]{:S(2)}) async-start(f32[64,1,16,128]{3,0,1,2:T(8,128)} %convolution_bitcast_fusion.4), calls=%async_computation.4 | async-start | bytes 1048576 | tf_op jit(solution)/shard_map/all_to_all | solution.py:79
  128.6 28.6 %copy-start.1 = (f32[128]{0:T(128)S(1)}, f32[128]{0:T(128)}, u32[]{:S(2)}) copy-start(f32[128]{0:T(128)} %param.6) | copy-start | bytes 1540
  128.6 45.4 %copy-start = (f32[64,128]{1,0:T(8,128)S(1)}, f32[64,128]{1,0:T(8,128)}, u32[]{:S(2)}) copy-start(f32[64,128]{1,0:T(8,128)} %param.5) | copy-start | bytes 98308
  147.6 26.4 %all-to-all-start.5 = ((f32[16,64,1,1,128]{4,1,3,2,0:T(8,128)}), f32[16,64,1,1,128]{4,1,3,2,0:T(8,128)S(1)}, u32[]{:S(2)}, u32[]{:S(2)}) async-start(f32[16,64,1,1,128]{4,1,3,2,0:T(8,128)} %bitcast.17), calls=%async_computation.5 | async-start | bytes 1048576 | tf_op jit(solution)/shard_map/all_to_all | solution.py:35
  186.8 17.9 %all-to-all-start.6 = ((bf16[16,64,128]{2,1,0:T(8,128)(2,1)}), bf16[16,64,128]{2,1,0:T(8,128)(2,1)}, u32[]{:S(2)}, u32[]{:S(2)}) async-start(bf16[16,64,128]{2,1,0:T(8,128)(2,1)} %broadcast_in_dim.22), calls=%async_computation.6 | async-start | bytes 524288 | tf_op jit(solution)/shard_map/all_to_all | solution.py:21
  204.7 12.0 %all-to-all-start.7 = ((bf16[64,16,1,128]{3,0,2,1:T(8,128)(2,1)}), bf16[64,16,1,128]{3,0,2,1:T(8,128)(2,1)S(1)}, u32[]{:S(2)}, u32[]{:S(2)}) async-start(bf16[64,16,1,128]{3,0,2,1:T(8,128)(2,1)} %bitcast.20), calls=%async_computation.7 | async-start | bytes 524288 | tf_op jit(solution)/shard_map/all_to_all | solution.py:72
  216.6 14.1 %all-to-all-start.10 = ((f32[64,1,16,128]{3,0,1,2:T(8,128)}), f32[64,1,16,128]{3,0,1,2:T(8,128)}, u32[]{:S(2)}, u32[]{:S(2)}) async-start(f32[64,1,16,128]{3,0,1,2:T(8,128)} %convolution_bitcast_fusion.2), calls=%async_computation.10 | async-start | bytes 1048576 | tf_op jit(solution)/shard_map/all_to_all | solution.py:79
  244.1 19.9 %all-to-all-start.11 = ((f32[16,64,1,1,128]{4,1,3,2,0:T(8,128)}), f32[16,64,1,1,128]{4,1,3,2,0:T(8,128)S(1)}, u32[]{:S(2)}, u32[]{:S(2)}) async-start(f32[16,64,1,1,128]{4,1,3,2,0:T(8,128)} %bitcast.27), calls=%async_computation.11 | async-start | bytes 1048576 | tf_op jit(solution)/shard_map/all_to_all | solution.py:35
  277.7 18.0 %all-to-all-start.12 = ((bf16[16,64,128]{2,1,0:T(8,128)(2,1)}), bf16[16,64,128]{2,1,0:T(8,128)(2,1)}, u32[]{:S(2)}, u32[]{:S(2)}) async-start(bf16[16,64,128]{2,1,0:T(8,128)(2,1)} %broadcast_in_dim.40), calls=%async_computation.12 | async-start | bytes 524288 | tf_op jit(solution)/shard_map/all_to_all | solution.py:21
  295.7 12.0 %all-to-all-start.13 = ((bf16[64,16,1,128]{3,0,2,1:T(8,128)(2,1)}), bf16[64,16,1,128]{3,0,2,1:T(8,128)(2,1)S(1)}, u32[]{:S(2)}, u32[]{:S(2)}) async-start(bf16[64,16,1,128]{3,0,2,1:T(8,128)(2,1)} %bitcast.30), calls=%async_computation.13 | async-start | bytes 524288 | tf_op jit(solution)/shard_map/all_to_all | solution.py:72
  307.6 14.1 %all-to-all-start.16 = ((f32[64,1,16,128]{3,0,1,2:T(8,128)}), f32[64,1,16,128]{3,0,1,2:T(8,128)}, u32[]{:S(2)}, u32[]{:S(2)}) async-start(f32[64,1,16,128]{3,0,1,2:T(8,128)} %convolution_bitcast_fusion), calls=%async_computation.16 | async-start | bytes 1048576 | tf_op jit(solution)/shard_map/all_to_all | solution.py:79
  335.1 19.9 %all-to-all-start.17 = ((f32[16,64,1,1,128]{4,1,3,2,0:T(8,128)}), f32[16,64,1,1,128]{4,1,3,2,0:T(8,128)S(1)}, u32[]{:S(2)}, u32[]{:S(2)}) async-start(f32[16,64,1,1,128]{4,1,3,2,0:T(8,128)} %bitcast.37), calls=%async_computation.17 | async-start | bytes 1048576 | tf_op jit(solution)/shard_map/all_to_all | solution.py:35
where the time goes:
time: 362 us; the launch traced here: 356 us
  waiting for transfers between devices  85.1 us (24%)
  starting transfers between devices  76.6 us (21%)
  blocking collectives  65.3 us (18%)
  local copies, waits for them, and re-layouts  58.6 us (16%)
  matrix products  35.3 us (10%)
  other arithmetic  33.9 us (9%)
    all_to_all x3, waiting for transfers between devices, summed_on_arrival(): lax.all_to_all(blocks, axis, split_axis=0, concat_axis=0, tiled=True)  48.7 us
    all_to_all x3, blocking collectives, summed_on_arrival(): lax.all_to_all(blocks, axis, split_axis=0, concat_axis=0, tiled=True)  40.5 us
    all_to_all x4, waiting for transfers between devices, sent_to_all(): return lax.all_to_all(copies, axis, split_axis=0, concat_axis=0, tiled=True)  30.1 us
    scatter-add x1, other arithmetic, build_tile(): placed = empty.at[row_places, col_places].add(masked)  27 us
    transpose x2, local copies, waits for them, and re-layouts, build_tile(): placed.transpose(0, 2, 1, 3)  26 us
    all_to_all x4, starting transfers between devices, sent_to_all(): return lax.all_to_all(copies, axis, split_axis=0, concat_axis=0, tiled=True)  25.6 us
    all_to_all x2, blocking collectives, sent_to_all(): return lax.all_to_all(copies, axis, split_axis=0, concat_axis=0, tiled=True)  24.8 us
    dot_general x3, matrix products, per_device(): transposed = jnp.dot(v_rows, tile, preferred_element_type=jnp.float32)  20.6 us
  transfers between devices with their start and end apart: 13, of which 8 were waited for; matrix products, arithmetic and copies ran while one was open for 35% of the time, Pallas kernels for 0%

commit v1 on v0

v1 whole, which is shorter than its diff:
```python
import functools

import jax
import jax.numpy as jnp
from jax import lax
from jax.experimental import pallas as pl
from jax.experimental.pallas import tpu as pltpu
from jax.sharding import PartitionSpec as P

STEPS = 3
G = 16
B = 128
V = 64
S = 128
MESH = pl.DeviceIdType.MESH

center_shift = 0.5
half_width = 3.0


def kernel(table, x_ref, scale_ref, blocks_hbm, out_ref, blk, tile, cur, prev, piece, vrow, vcol, dsend, tsend, drecv, trecv,
           blk_sem, send_sem, recv_sem):
    r = lax.axis_index("row")
    c = lax.axis_index("col")
    diag = r == c

    load = pltpu.make_async_copy(blocks_hbm, blk.at[pl.ds(0, S)], blk_sem)
    load.start()

    barrier = pltpu.get_barrier_semaphore()

    def signal(row, col):
        pl.semaphore_signal(barrier, inc=1, device_id=(row, col), device_id_type=MESH)

    def greet(k, _):
        signal(lax.rem(r + k, G), r)
        signal(r, lax.rem(c + k, G))
        return 0

    lax.fori_loop(1, G, greet, 0)

    @pl.when(jnp.logical_not(diag))
    def _():
        def greet_col(k, _):
            signal(c, lax.rem(r + k, G))
            return 0

        lax.fori_loop(1, G, greet_col, 0)

    cur[...] = x_ref[...]
    prev[...] = jnp.zeros((V, B), jnp.float32)
    blk[S] = jnp.zeros((B, B), jnp.bfloat16)
    load.wait()

    def build(i, _):
        for j in range(G):
            tile[pl.ds(pl.multiple_of(i * B, B), B), pl.ds(j * B, B)] = blk[table[i * G + j]]
        return 0

    lax.fori_loop(0, G, build, 0)

    pl.semaphore_wait(barrier, jnp.where(diag, 2, 3) * (G - 1))

    def post(src, dst, kind, step, row, col):
        own = jnp.logical_and(row == r, col == c)

        @pl.when(own)
        def _():
            pltpu.make_async_copy(src, dst, recv_sem.at[kind, step]).start()

        @pl.when(jnp.logical_not(own))
        def _():
            pltpu.make_async_remote_copy(src, dst, send_sem.at[kind, step], recv_sem.at[kind, step], device_id=(row, col),
                                         device_id_type=MESH).start()

    def arrive(buf, kind, step):
        pltpu.make_async_copy(buf.at[step], buf.at[step], recv_sem.at[kind, step]).wait()

    def one_step(step, _):
        scale = scale_ref[...]
        piece[step] = (scale * cur[...]).astype(jnp.bfloat16)

        def share_cols(k, _):
            post(piece.at[step], vcol.at[step, c], 1, step, lax.rem(r + k, G), r)
            return 0

        def share_rows(k, _):
            post(piece.at[step], vrow.at[step, c], 0, step, r, lax.rem(c + k, G))
            return 0

        lax.fori_loop(0, G, share_rows, 0)
        lax.fori_loop(0, G, share_cols, 0)

        arrive(vrow, 0, step)

        def transposed(n, _):
            acc = jnp.zeros((V, 2 * B), jnp.float32)
            for k in range(G // 2):
                v = jnp.concatenate([vrow[step, 2 * k], vrow[step, 2 * k + 1]], axis=1)
                w = tile[pl.ds(2 * k * B, 2 * B), pl.ds(pl.multiple_of(n * 2 * B, 2 * B), 2 * B)]
                acc += jnp.dot(v, w, preferred_element_type=jnp.float32)
            for u in range(2):
                j = 2 * n + u
                tsend[step, j] = acc[:, u * B : (u + 1) * B].astype(jnp.bfloat16)
                post(tsend.at[step, j], trecv.at[step, r], 2, step, c, j)
            return 0

        lax.fori_loop(0, G // 2, transposed, 0)

        arrive(vcol, 1, step)

        def direct(n, _):
            acc = jnp.zeros((V, 2 * B), jnp.float32)
            for k in range(G // 2):
                v = jnp.concatenate([vcol[step, 2 * k], vcol[step, 2 * k + 1]], axis=1)
                w = tile[pl.ds(pl.multiple_of(n * 2 * B, 2 * B), 2 * B), pl.ds(2 * k * B, 2 * B)]
                acc += lax.dot_general(v, w, (((1,), (1,)), ((), ())), preferred_element_type=jnp.float32)
            for u in range(2):
                j = 2 * n + u
                dsend[step, j] = acc[:, u * B : (u + 1) * B].astype(jnp.bfloat16)
                post(dsend.at[step, j], drecv.at[step, c], 3, step, r, j)
            return 0

        lax.fori_loop(0, G // 2, direct, 0)

        arrive(trecv, 2, step)
        arrive(drecv, 3, step)
        applied = jnp.zeros((V, B), jnp.float32)
        for k in range(G):
            applied += trecv[step, k].astype(jnp.float32)
            applied += drecv[step, k].astype(jnp.float32)
        now = cur[...]
        mapped = scale * applied - center_shift * now
        first = step == 0
        factor = jnp.where(first, 1.0 / half_width, 2.0 / half_width)
        updated = factor * mapped - prev[...]
        prev[...] = now
        cur[...] = updated
        return 0

    lax.fori_loop(0, STEPS, one_step, 0)
    out_ref[...] = cur[...]

    def drain(step, _):
        for kind, buf in enumerate((vrow, vcol, tsend, dsend)):
            sent = buf.at[step, pl.ds(0, G - 1)]
            pltpu.make_async_copy(sent, sent, send_sem.at[kind, step]).wait()

        @pl.when(jnp.logical_not(diag))
        def _():
            for kind, buf in ((1, vcol), (2, tsend)):
                sent = buf.at[step, pl.ds(0, 1)]
                pltpu.make_async_copy(sent, sent, send_sem.at[kind, step]).wait()

        return 0

    lax.fori_loop(0, STEPS, drain, 0)


def per_device(start_vectors, scaling, block_values, block_places, block_counts):
    blocks = block_values.reshape(S, B, B)
    places = block_places.reshape(2, S)
    slots = jnp.arange(S, dtype=jnp.int32)
    at = jnp.where(slots < block_counts.reshape(()), places[0] * G + places[1], -1)
    hit = at[None, :] == jnp.arange(G * G, dtype=jnp.int32)[:, None]
    table = jnp.min(jnp.where(hit, slots[None, :], S), axis=1)
    vmem = pl.BlockSpec(memory_space=pltpu.VMEM)
    slab = pltpu.VMEM((STEPS, G, V, B), jnp.bfloat16)
    return pl.pallas_call(
        kernel,
        name="filter",
        out_shape=jax.ShapeDtypeStruct((V, B), jnp.float32),
        in_specs=[pl.BlockSpec(memory_space=pltpu.SMEM), vmem, vmem, pl.BlockSpec(memory_space=pl.ANY)],
        out_specs=vmem,
        scratch_shapes=[
            pltpu.VMEM((S + 1, B, B), jnp.bfloat16),
            pltpu.VMEM((G * B, G * B), jnp.bfloat16),
            pltpu.VMEM((V, B), jnp.float32),
            pltpu.VMEM((V, B), jnp.float32),
            pltpu.VMEM((STEPS, V, B), jnp.bfloat16),
            slab, slab, slab, slab, slab, slab,
            pltpu.SemaphoreType.DMA,
            pltpu.SemaphoreType.DMA((4, STEPS)),
            pltpu.SemaphoreType.DMA((4, STEPS)),
        ],
        compiler_params=pltpu.CompilerParams(collective_id=0, has_side_effects=True, vmem_limit_bytes=48 << 20),
    )(table, start_vectors, scaling.reshape(1, B), blocks)


def solution(mesh):
    in_specs = (
        P(None, ("row", "col")),
        P(("row", "col")),
        P("row", "col", None, None, None),
        P("row", "col", None, None),
        P("row", "col"),
    )
    out_specs = P(None, ("row", "col"))
    return jax.shard_map(
        per_device, mesh=mesh, in_specs=in_specs, out_specs=out_specs, check_vma=False
    )
```

time: 362 us -> 104 us (0.29)
  the two profiles are of different devices: /device:TPU:8 before, /device:TPU:63 now
where the time goes in v1:
time: 104 us
  Pallas kernels  98.3 us (95%)
  local copies, waits for them, and re-layouts  4.21 us (4%)
    pallas_call x1, Pallas kernels, per_device(): pl.pallas_call(kernel, name='filter', out_shape=jax.ShapeDtypeStruct((V,...  98.3 us
    unnamed x7, local copies, waits for them, and re-layouts  4.21 us

profile of v1, /device:TPU:63, one launch (start us, length us, event | category | flops | bytes accessed | tf_op | source)
XLA Modules:
  0.0 104.0 jit_solution(3286913584035390945)
XLA Ops:
  0.7 0.8 compare_select_fusion
  1.4 0.1 select_reduce_fusion.table
  1.5 0.0 copy-start
  1.5 2.2 %copy-done = bf16[1,1,128,128,128]{4,3,2,1,0:T(8,128)(2,1)S(1)} copy-done((bf16[1,1,128,128,128]{4,3,2,1,0:T(8,128)(2,1)S(1)}, bf16[1,1,128,128,128]{4,3,2,1,0:T(8,128)(2,1)}, u32[]{:S(2)}) %copy-start) | copy-done | bytes 4194328
  3.7 0.0 copy-start.1
  3.7 0.8 copy-done.1
  4.5 0.0 copy-start.2
  4.5 0.7 copy-done.2
  5.1 98.3 %filter.1 = f32[64,128]{1,0:T(8,128)S(1)} custom-call(s32[256]{0:T(256)S(1)} %select_reduce_fusion.table, f32[64,128]{1,0:T(8,128)S(1)} %copy-done.1, f32[1,128]{1,0:T(1,128)S(1)} %bitcast.7, bf16[128,128,128]{2,1,0:T(8,128)(2,1)S(1)} %bitcast.6), custom_call_target="tpu_custom_call" | custom-call | tf_op jit(solution)/shard_map/filter/pallas_call | solution.py:169
  103.4 0.6 copy.8
Async XLA Ops:
  1.5 2.2 %copy-start = (bf16[1,1,128,128,128]{4,3,2,1,0:T(8,128)(2,1)S(1)}, bf16[1,1,128,128,128]{4,3,2,1,0:T(8,128)(2,1)}, u32[]{:S(2)}) copy-start(bf16[1,1,128,128,128]{4,3,2,1,0:T(8,128)(2,1)} %param.7) | copy-start | bytes 12582916
  3.7 0.8 copy-start.1
  4.5 0.7 copy-start.2

commit v2 on v1

v2 whole, which is shorter than its diff:
```python
import jax
import jax.numpy as jnp
from jax import lax
from jax.experimental import pallas as pl
from jax.experimental.pallas import tpu as pltpu
from jax.sharding import PartitionSpec as P

STEPS = 3
G = 16
Q = 4
B = 128
V = 64
S = 128
MESH = pl.DeviceIdType.MESH
VROW, HOP, VCOL, PART, SUMS, DIRECT = range(6)

center_shift = 0.5
half_width = 3.0


def kernel(x_hbm, scale_hbm, places_hbm, count_hbm, blocks_hbm, out_ref, blk, tile, cur, prev, scale_ref, places, count,
           table_v, table, piece, hop, vrow, vcol, tsend, dsend, part, sums_send, sums, drecv, in_sem, send_sem, recv_sem,
           hop_sem):
    r = lax.axis_index("row")
    c = lax.axis_index("col")
    r_hi, r_lo = r // Q, lax.rem(r, Q)
    c_hi, c_lo = c // Q, lax.rem(c, Q)
    home = r_lo == c_lo

    loads = [
        pltpu.make_async_copy(src, dst, in_sem.at[i])
        for i, (src, dst) in enumerate(((x_hbm, cur), (scale_hbm, scale_ref), (places_hbm, places), (count_hbm, count),
                                        (blocks_hbm, blk.at[pl.ds(0, S)])))
    ]
    for load in loads:
        load.start()

    barrier = pltpu.get_barrier_semaphore()

    def signal(row, col):
        pl.semaphore_signal(barrier, inc=1, device_id=(row, col), device_id_type=MESH)

    def greet_row(k, _):
        signal(r, lax.rem(c + k, G))
        return 0

    lax.fori_loop(1, G, greet_row, 0)
    for k in range(1, Q):
        signal(lax.rem(r + Q * k, G), c)

    def greet_plane(k, _):
        row = r_hi * Q + lax.rem(r_lo + 1 + k // Q, Q)
        signal(row, lax.rem(k, Q) * Q + r_lo)
        return 0

    lax.fori_loop(0, Q * (Q - 1), greet_plane, 0)

    @pl.when(jnp.logical_not(home))
    def _():
        def greet_other(k, _):
            lo = lax.rem(r_lo + 1 + lax.rem(k, Q - 1), Q)
            signal(r_hi * Q + c_lo, (k // (Q - 1)) * Q + lo)
            return 0

        lax.fori_loop(0, Q * (Q - 1), greet_other, 0)

    prev[...] = jnp.zeros((V, B), jnp.float32)
    blk[S] = jnp.zeros((B, B), jnp.bfloat16)

    loads[2].wait()
    loads[3].wait()
    lane = lax.broadcasted_iota(jnp.int32, (1, S), 1)
    at = jnp.where(lane < count[...], places[0:1, :] * G + places[1:2, :], -1)
    row_id = lax.broadcasted_iota(jnp.int32, (S, S), 0)
    col_id = lax.broadcasted_iota(jnp.int32, (S, S), 1)
    for half in range(2):
        slot = jnp.min(jnp.where(row_id + half * S == at, col_id, S), axis=1, keepdims=True)
        table_v[half : half + 1, :] = jnp.min(jnp.where(row_id == col_id, slot, S), axis=0, keepdims=True)
    to_scalars = pltpu.make_async_copy(table_v, table, in_sem.at[5])
    to_scalars.start()
    loads[0].wait()
    loads[1].wait()

    pl.semaphore_wait(barrier, jnp.where(home, 15 + 3 + 12, 15 + 3 + 12 + 12))

    def post(src, dst, kind, step, row, col):
        own = jnp.logical_and(row == r, col == c)

        @pl.when(own)
        def _():
            pltpu.make_async_copy(src, dst, recv_sem.at[kind, step]).start()

        @pl.when(jnp.logical_not(own))
        def _():
            pltpu.make_async_remote_copy(src, dst, send_sem.at[kind, step], recv_sem.at[kind, step], device_id=(row, col),
                                         device_id_type=MESH).start()

    def arrive(buf, kind, step):
        pltpu.make_async_copy(buf.at[step], buf.at[step], recv_sem.at[kind, step]).wait()

    def share(step):
        piece[step] = (scale_ref[...] * cur[...]).astype(jnp.bfloat16)

        def along_row(k, _):
            post(piece.at[step], vrow.at[step, c], VROW, step, r, lax.rem(c + k, G))
            return 0

        def hop_to(k):
            return pltpu.make_async_remote_copy(piece.at[step], hop.at[step, k - 1], send_sem.at[HOP, step],
                                                hop_sem.at[step, k - 1], device_id=(lax.rem(r + Q * k, G), c),
                                                device_id_type=MESH)

        def spread(src, k):
            col = lax.rem(r_hi + Q - k, Q) * Q + r_lo

            def to(i, _):
                post(src, vcol.at[step, c], VCOL, step, r_hi * Q + lax.rem(r_lo + i, Q), col)
                return 0

            lax.fori_loop(0, Q, to, 0)

        hops = [hop_to(k) for k in (2, 1, 3)]
        for h in hops:
            h.start()
        lax.fori_loop(0, G, along_row, 0)
        spread(piece.at[step], 0)
        for k in (1, 3, 2):
            pltpu.make_async_copy(hop.at[step, k - 1], hop.at[step, k - 1], hop_sem.at[step, k - 1]).wait()
            spread(hop.at[step, k - 1], k)

    def multiply(step):
        with jax.named_scope("wait_vrow"):
            arrive(vrow, VROW, step)

        def transposed(n, _):
            acc = jnp.zeros((V, 2 * B), jnp.float32)
            for k in range(G // 2):
                v = jnp.concatenate([vrow[step, 2 * k], vrow[step, 2 * k + 1]], axis=1)
                w = tile[pl.ds(2 * k * B, 2 * B), pl.ds(pl.multiple_of(n * 2 * B, 2 * B), 2 * B)]
                acc += jnp.dot(v, w, preferred_element_type=jnp.float32)
            for u in range(2):
                j = 2 * n + u
                tsend[step, j] = acc[:, u * B : (u + 1) * B].astype(jnp.bfloat16)
                post(tsend.at[step, j], part.at[step, r_lo * Q + c_hi], PART, step, r_hi * Q + c_lo, j)
            return 0

        with jax.named_scope("mm_transposed"):
            lax.fori_loop(0, G // 2, transposed, 0)

        with jax.named_scope("wait_vcol"):
            arrive(vcol, VCOL, step)

        def direct(n, _):
            acc = jnp.zeros((V, 2 * B), jnp.float32)
            for k in range(G // 2):
                v = jnp.concatenate([vcol[step, 2 * k], vcol[step, 2 * k + 1]], axis=1)
                w = tile[pl.ds(pl.multiple_of(n * 2 * B, 2 * B), 2 * B), pl.ds(2 * k * B, 2 * B)]
                acc += lax.dot_general(v, w, (((1,), (1,)), ((), ())), preferred_element_type=jnp.float32)
            for u in range(2):
                j = 2 * n + u
                dsend[step, j] = acc[:, u * B : (u + 1) * B].astype(jnp.bfloat16)
                post(dsend.at[step, j], drecv.at[step, c], DIRECT, step, r, j)
            return 0

        with jax.named_scope("mm_direct"):
            lax.fori_loop(0, G // 2, direct, 0)

    def collect(step):
        with jax.named_scope("wait_part"):
            arrive(part, PART, step)
        for k in (2, 1, 3, 0):
            hi = lax.rem(r_hi + k, Q)
            total = jnp.zeros((V, B), jnp.float32)
            for lo in range(Q):
                total += part[step, lo * Q + hi].astype(jnp.float32)
            if k == 0:
                applied = total
            else:
                sums_send[step, k - 1] = total.astype(jnp.bfloat16)
                pltpu.make_async_remote_copy(sums_send.at[step, k - 1], sums.at[step, k - 1], send_sem.at[SUMS, step],
                                             recv_sem.at[SUMS, step], device_id=(hi * Q + r_lo, c),
                                             device_id_type=MESH).start()
        with jax.named_scope("wait_drecv"):
            arrive(drecv, DIRECT, step)
        for k in range(G):
            applied += drecv[step, k].astype(jnp.float32)
        with jax.named_scope("wait_sums"):
            arrive(sums, SUMS, step)
        for k in range(Q - 1):
            applied += sums[step, k].astype(jnp.float32)
        now = cur[...]
        mapped = scale_ref[...] * applied - center_shift * now
        factor = jnp.where(step == 0, 1.0 / half_width, 2.0 / half_width)
        updated = factor * mapped - prev[...]
        prev[...] = now
        cur[...] = updated

    def one_step(step, _):
        with jax.named_scope("share"):
            share(step)

        @pl.when(step == 0)
        def _():
            with jax.named_scope("build"):
                to_scalars.wait()
                loads[4].wait()

                def build(i, _):
                    for j in range(G):
                        slot = jnp.clip(table[i // 8, lax.rem(i, 8) * G + j], 0, S)
                        tile[pl.ds(pl.multiple_of(i * B, B), B), pl.ds(j * B, B)] = blk[slot]
                    return 0

                lax.fori_loop(0, G, build, 0)

        multiply(step)
        collect(step)
        return 0

    lax.fori_loop(0, STEPS, one_step, 0)
    out_ref[...] = cur[...]

    def drain(step, _):
        for kind, buf, n in ((VROW, vrow, G - 1), (HOP, hop, Q - 1), (VCOL, vcol, G - 1), (PART, part, G - 1),
                             (SUMS, sums, Q - 1), (DIRECT, drecv, G - 1)):
            sent = buf.at[step, pl.ds(0, n)]
            pltpu.make_async_copy(sent, sent, send_sem.at[kind, step]).wait()

        @pl.when(jnp.logical_not(home))
        def _():
            for kind, buf in ((VCOL, vcol), (PART, part)):
                sent = buf.at[step, pl.ds(0, 1)]
                pltpu.make_async_copy(sent, sent, send_sem.at[kind, step]).wait()

        return 0

    with jax.named_scope("drain"):
        lax.fori_loop(0, STEPS, drain, 0)


def per_device(start_vectors, scaling, block_values, block_places, block_counts):
    anywhere = pl.BlockSpec(memory_space=pl.ANY)

    def slab(n):
        return pltpu.VMEM((STEPS, n, V, B), jnp.bfloat16)

    f32 = pltpu.VMEM((V, B), jnp.float32)
    return pl.pallas_call(
        kernel,
        name="filter",
        out_shape=jax.ShapeDtypeStruct((V, B), jnp.float32),
        in_specs=[anywhere] * 5,
        out_specs=pl.BlockSpec(memory_space=pltpu.VMEM),
        scratch_shapes=[
            pltpu.VMEM((S + 1, B, B), jnp.bfloat16),
            pltpu.VMEM((G * B, G * B), jnp.bfloat16),
            f32,
            f32,
            pltpu.VMEM((1, B), jnp.float32),
            pltpu.VMEM((2, S), jnp.int32),
            pltpu.VMEM((1, 1), jnp.int32),
            pltpu.VMEM((2, S), jnp.int32),
            pltpu.SMEM((2, S), jnp.int32),
            pltpu.VMEM((STEPS, V, B), jnp.bfloat16),
            slab(Q - 1), slab(G), slab(G), slab(G), slab(G), slab(G), slab(Q - 1), slab(Q - 1), slab(G),
            pltpu.SemaphoreType.DMA((6,)),
            pltpu.SemaphoreType.DMA((6, STEPS)),
            pltpu.SemaphoreType.DMA((6, STEPS)),
            pltpu.SemaphoreType.DMA((STEPS, Q - 1)),
        ],
        compiler_params=pltpu.CompilerParams(collective_id=0, has_side_effects=True, vmem_limit_bytes=60 << 20),
    )(start_vectors, scaling.reshape(1, B), block_places.reshape(2, S), block_counts, block_values.reshape(S, B, B))


def solution(mesh):
    in_specs = (
        P(None, ("row", "col")),
        P(("row", "col")),
        P("row", "col", None, None, None),
        P("row", "col", None, None),
        P("row", "col"),
    )
    out_specs = P(None, ("row", "col"))
    return jax.shard_map(
        per_device, mesh=mesh, in_specs=in_specs, out_specs=out_specs, check_vma=False
    )
```

time: 104 us -> 82.6 us (0.79)
  the two profiles are of different devices: /device:TPU:63 before, /device:TPU:8 now
where the time goes in v2:
time: 82.6 us; the launch traced here: 80.9 us
  Pallas kernels  78.9 us (96%)
  local copies, waits for them, and re-layouts  1.38 us (2%)
    pallas_call x1, Pallas kernels, per_device(): pl.pallas_call(kernel, name='filter', out_shape=jax.ShapeDtypeStruct((V,...  78.9 us

profile of v2, /device:TPU:8, one launch (start us, length us, event | category | flops | bytes accessed | tf_op | source)
XLA Modules:
  0.0 80.9 jit_solution(252207145009658078)
XLA Ops:
  0.7 78.9 %filter.1 = f32[64,128]{1,0:T(8,128)} custom-call(f32[64,128]{1,0:T(8,128)} %x_hbm.1, f32[1,128]{1,0:T(1,128)} %bitcast.5, s32[2,128]{1,0:T(2,128)} %bitcast.4, s32[1,1]{1,0:T(1,128)S(6)} %copy.7.count_hbm, bf16[128,128,128]{2,1,0:T(8,128)(2,1)} %bitcast.3), custom_call_target="tpu_custom_call" | custom-call | tf_op jit(solution)/shard_map/filter/pallas_call | solution.py:248
  79.5 1.4 %copy.8 = f32[64,128]{1,0:T(8,128)} copy(f32[64,128]{1,0:T(8,128)} %filter.1) | data formatting | bytes 65536

commit v3 on v2

--- a/solution.py
+++ b/solution.py
@@ -25,7 +25,7 @@
     c = lax.axis_index("col")
     r_hi, r_lo = r // Q, lax.rem(r, Q)
     c_hi, c_lo = c // Q, lax.rem(c, Q)
-    home = r_lo == c_lo
+    home_hi, home_lo = r_hi == c_hi, r_lo == c_lo
 
     loads = [
         pltpu.make_async_copy(src, dst, in_sem.at[i])
@@ -40,29 +40,25 @@
     def signal(row, col):
         pl.semaphore_signal(barrier, inc=1, device_id=(row, col), device_id_type=MESH)
 
+    for k in range(1, Q):
+        signal(lax.rem(r_hi + k, Q) * Q + r_lo, r_hi * Q + c_lo)
+        signal(r_hi * Q + lax.rem(r_lo + k, Q), c_hi * Q + r_lo)
+
+    @pl.when(jnp.logical_not(home_hi))
+    def _():
+        for k in range(1, Q):
+            signal(c_hi * Q + r_lo, lax.rem(r_hi + k, Q) * Q + c_lo)
+
+    @pl.when(jnp.logical_not(home_lo))
+    def _():
+        for k in range(1, Q):
+            signal(r_hi * Q + c_lo, c_hi * Q + lax.rem(r_lo + k, Q))
+
     def greet_row(k, _):
         signal(r, lax.rem(c + k, G))
         return 0
 
     lax.fori_loop(1, G, greet_row, 0)
-    for k in range(1, Q):
-        signal(lax.rem(r + Q * k, G), c)
-
-    def greet_plane(k, _):
-        row = r_hi * Q + lax.rem(r_lo + 1 + k // Q, Q)
-        signal(row, lax.rem(k, Q) * Q + r_lo)
-        return 0
-
-    lax.fori_loop(0, Q * (Q - 1), greet_plane, 0)
-
-    @pl.when(jnp.logical_not(home))
-    def _():
-        def greet_other(k, _):
-            lo = lax.rem(r_lo + 1 + lax.rem(k, Q - 1), Q)
-            signal(r_hi * Q + c_lo, (k // (Q - 1)) * Q + lo)
-            return 0
-
-        lax.fori_loop(0, Q * (Q - 1), greet_other, 0)
 
     prev[...] = jnp.zeros((V, B), jnp.float32)
     blk[S] = jnp.zeros((B, B), jnp.bfloat16)
@@ -80,19 +76,33 @@
     to_scalars.start()
     loads[0].wait()
     loads[1].wait()
-
-    pl.semaphore_wait(barrier, jnp.where(home, 15 + 3 + 12, 15 + 3 + 12 + 12))
-
-    def post(src, dst, kind, step, row, col):
+    with jax.named_scope("load"):
+        loads[4].wait()
+        to_scalars.wait()
+
+    def build(i, _):
+        for j in range(G):
+            slot = jnp.clip(table[i // 8, lax.rem(i, 8) * G + j], 0, S)
+            tile[pl.ds(pl.multiple_of(i * B, B), B), pl.ds(j * B, B)] = blk[slot]
+        return 0
+
+    with jax.named_scope("build"):
+        lax.fori_loop(0, G, build, 0)
+
+    with jax.named_scope("barrier"):
+        pl.semaphore_wait(barrier, G - 1 + jnp.where(home_hi, 3, 6) + jnp.where(home_lo, 3, 6))
+
+    def post(src, dst, kind, step, row, col, arrival=None):
         own = jnp.logical_and(row == r, col == c)
+        arrival = recv_sem.at[kind, step] if arrival is None else arrival
 
         @pl.when(own)
         def _():
-            pltpu.make_async_copy(src, dst, recv_sem.at[kind, step]).start()
+            pltpu.make_async_copy(src, dst, arrival).start()
 
         @pl.when(jnp.logical_not(own))
         def _():
-            pltpu.make_async_remote_copy(src, dst, send_sem.at[kind, step], recv_sem.at[kind, step], device_id=(row, col),
+            pltpu.make_async_remote_copy(src, dst, send_sem.at[kind, step], arrival, device_id=(row, col),
                                          device_id_type=MESH).start()
 
     def arrive(buf, kind, step):
@@ -105,28 +115,19 @@
             post(piece.at[step], vrow.at[step, c], VROW, step, r, lax.rem(c + k, G))
             return 0
 
-        def hop_to(k):
-            return pltpu.make_async_remote_copy(piece.at[step], hop.at[step, k - 1], send_sem.at[HOP, step],
-                                                hop_sem.at[step, k - 1], device_id=(lax.rem(r + Q * k, G), c),
-                                                device_id_type=MESH)
-
-        def spread(src, k):
-            col = lax.rem(r_hi + Q - k, Q) * Q + r_lo
-
-            def to(i, _):
-                post(src, vcol.at[step, c], VCOL, step, r_hi * Q + lax.rem(r_lo + i, Q), col)
+        for k in (2, 1, 3, 0):
+            row, col = lax.rem(r_hi + k, Q) * Q + r_lo, r_hi * Q + c_lo
+            post(piece.at[step], hop.at[step, c_hi], HOP, step, row, col, hop_sem.at[step, c_hi])
+        lax.fori_loop(0, G, along_row, 0)
+        for k in (0, 1, 3, 2):
+            hi = lax.rem(c_hi + k, Q)
+            pltpu.make_async_copy(hop.at[step, hi], hop.at[step, hi], hop_sem.at[step, hi]).wait()
+
+            def spread(i, _):
+                post(hop.at[step, hi], vcol.at[step, hi * Q + c_lo], VCOL, step, r_hi * Q + lax.rem(r_lo + i, Q), c_hi * Q + r_lo)
                 return 0
 
-            lax.fori_loop(0, Q, to, 0)
-
-        hops = [hop_to(k) for k in (2, 1, 3)]
-        for h in hops:
-            h.start()
-        lax.fori_loop(0, G, along_row, 0)
-        spread(piece.at[step], 0)
-        for k in (1, 3, 2):
-            pltpu.make_async_copy(hop.at[step, k - 1], hop.at[step, k - 1], hop_sem.at[step, k - 1]).wait()
-            spread(hop.at[step, k - 1], k)
+            lax.fori_loop(0, Q, spread, 0)
 
     def multiply(step):
         with jax.named_scope("wait_vrow"):
@@ -141,7 +142,8 @@
             for u in range(2):
                 j = 2 * n + u
                 tsend[step, j] = acc[:, u * B : (u + 1) * B].astype(jnp.bfloat16)
-                post(tsend.at[step, j], part.at[step, r_lo * Q + c_hi], PART, step, r_hi * Q + c_lo, j)
+                post(tsend.at[step, j], part.at[step, r_lo * Q + n // 2], PART, step, r_hi * Q + c_lo,
+                     c_hi * Q + 2 * lax.rem(n, 2) + u)
             return 0
 
         with jax.named_scope("mm_transposed"):
@@ -150,7 +152,8 @@
         with jax.named_scope("wait_vcol"):
             arrive(vcol, VCOL, step)
 
-        def direct(n, _):
+        def direct(i, _):
+            n = lax.rem(2 * c_hi + Q + i, G // 2)
             acc = jnp.zeros((V, 2 * B), jnp.float32)
             for k in range(G // 2):
                 v = jnp.concatenate([vcol[step, 2 * k], vcol[step, 2 * k + 1]], axis=1)
@@ -168,25 +171,21 @@
     def collect(step):
         with jax.named_scope("wait_part"):
             arrive(part, PART, step)
-        for k in (2, 1, 3, 0):
-            hi = lax.rem(r_hi + k, Q)
+        for k in range(Q):
+            hi = lax.rem(c_hi + 2 + k, Q)
             total = jnp.zeros((V, B), jnp.float32)
             for lo in range(Q):
                 total += part[step, lo * Q + hi].astype(jnp.float32)
-            if k == 0:
-                applied = total
-            else:
-                sums_send[step, k - 1] = total.astype(jnp.bfloat16)
-                pltpu.make_async_remote_copy(sums_send.at[step, k - 1], sums.at[step, k - 1], send_sem.at[SUMS, step],
-                                             recv_sem.at[SUMS, step], device_id=(hi * Q + r_lo, c),
-                                             device_id_type=MESH).start()
+            sums_send[step, k] = total.astype(jnp.bfloat16)
+            post(sums_send.at[step, k], sums.at[step, r_hi], SUMS, step, c_hi * Q + r_lo, hi * Q + c_lo)
+        applied = jnp.zeros((V, B), jnp.float32)
         with jax.named_scope("wait_drecv"):
             arrive(drecv, DIRECT, step)
         for k in range(G):
             applied += drecv[step, k].astype(jnp.float32)
         with jax.named_scope("wait_sums"):
             arrive(sums, SUMS, step)
-        for k in range(Q - 1):
+        for k in range(Q):
             applied += sums[step, k].astype(jnp.float32)
         now = cur[...]
         mapped = scale_ref[...] * applied - center_shift * now
@@ -199,20 +198,6 @@
         with jax.named_scope("share"):
             share(step)
 
-        @pl.when(step == 0)
-        def _():
-            with jax.named_scope("build"):
-                to_scalars.wait()
-                loads[4].wait()
-
-                def build(i, _):
-                    for j in range(G):
-                        slot = jnp.clip(table[i // 8, lax.rem(i, 8) * G + j], 0, S)
-                        tile[pl.ds(pl.multiple_of(i * B, B), B), pl.ds(j * B, B)] = blk[slot]
-                    return 0
-
-                lax.fori_loop(0, G, build, 0)
-
         multiply(step)
         collect(step)
         return 0
@@ -221,16 +206,19 @@
     out_ref[...] = cur[...]
 
     def drain(step, _):
-        for kind, buf, n in ((VROW, vrow, G - 1), (HOP, hop, Q - 1), (VCOL, vcol, G - 1), (PART, part, G - 1),
-                             (SUMS, sums, Q - 1), (DIRECT, drecv, G - 1)):
-            sent = buf.at[step, pl.ds(0, n)]
-            pltpu.make_async_copy(sent, sent, send_sem.at[kind, step]).wait()
-
-        @pl.when(jnp.logical_not(home))
-        def _():
-            for kind, buf in ((VCOL, vcol), (PART, part)):
-                sent = buf.at[step, pl.ds(0, 1)]
-                pltpu.make_async_copy(sent, sent, send_sem.at[kind, step]).wait()
+        def sent(kind, buf, n):
+            done = buf.at[step, pl.ds(0, n)]
+            pltpu.make_async_copy(done, done, send_sem.at[kind, step]).wait()
+
+        for kind, buf in ((VROW, vrow), (DIRECT, drecv)):
+            sent(kind, buf, G - 1)
+        for kind, buf, n, home, own in ((HOP, hop, Q, home_hi, 1), (SUMS, sums, Q, home_hi, 1), (VCOL, vcol, G, home_lo, Q),
+                                        (PART, part, G, home_lo, Q)):
+            sent(kind, buf, n - own)
+
+            @pl.when(jnp.logical_not(home))
+            def _():
+                sent(kind, buf, own)
 
         return 0
 
@@ -262,11 +250,11 @@
             pltpu.VMEM((2, S), jnp.int32),
             pltpu.SMEM((2, S), jnp.int32),
             pltpu.VMEM((STEPS, V, B), jnp.bfloat16),
-            slab(Q - 1), slab(G), slab(G), slab(G), slab(G), slab(G), slab(Q - 1), slab(Q - 1), slab(G),
+            slab(Q), slab(G), slab(G), slab(G), slab(G), slab(G), slab(Q), slab(Q), slab(G),
             pltpu.SemaphoreType.DMA((6,)),
             pltpu.SemaphoreType.DMA((6, STEPS)),
             pltpu.SemaphoreType.DMA((6, STEPS)),
-            pltpu.SemaphoreType.DMA((STEPS, Q - 1)),
+            pltpu.SemaphoreType.DMA((STEPS, Q)),
         ],
         compiler_params=pltpu.CompilerParams(collective_id=0, has_side_effects=True, vmem_limit_bytes=60 << 20),
     )(start_vectors, scaling.reshape(1, B), block_places.reshape(2, S), block_counts, block_values.reshape(S, B, B))

time: 82.6 us -> 85.6 us (1.036)
  Pallas kernels: 78.9 us -> 82.2 us
    pallas_call x1, Pallas kernels: 78.9 us -> 82.2 us  [per_device(): pl.pallas_call(kernel, name='filter', out_shape=jax.ShapeDtypeStruct((V,...]
where the time goes in v3:
time: 85.6 us; the launch traced here: 84.2 us
  Pallas kernels  82.2 us (96%)
  local copies, waits for them, and re-layouts  1.38 us (2%)
    pallas_call x1, Pallas kernels, per_device(): pl.pallas_call(kernel, name='filter', out_shape=jax.ShapeDtypeStruct((V,...  82.2 us

profile of v3, /device:TPU:8, one launch (start us, length us, event | category | flops | bytes accessed | tf_op | source)
XLA Modules:
  0.0 84.2 jit_solution(13959065944412707851)
XLA Ops:
  0.7 82.2 %filter.1 = f32[64,128]{1,0:T(8,128)} custom-call(f32[64,128]{1,0:T(8,128)} %x_hbm.1, f32[1,128]{1,0:T(1,128)} %bitcast.5, s32[2,128]{1,0:T(2,128)} %bitcast.4, s32[1,1]{1,0:T(1,128)S(6)} %copy.7.count_hbm, bf16[128,128,128]{2,1,0:T(8,128)(2,1)} %bitcast.3), custom_call_target="tpu_custom_call" | custom-call | tf_op jit(solution)/shard_map/filter/pallas_call | solution.py:236
  82.9 1.4 %copy.8 = f32[64,128]{1,0:T(8,128)} copy(f32[64,128]{1,0:T(8,128)} %filter.1) | data formatting | bytes 65536

commit v4 on v3

v4 whole, which is shorter than its diff:
```python
import jax
import jax.numpy as jnp
from jax import lax
from jax.experimental import pallas as pl
from jax.experimental.pallas import tpu as pltpu
from jax.sharding import PartitionSpec as P

STEPS = 3
G = 16
Q = 4
B = 128
V = 64
S = 128
MESH = pl.DeviceIdType.MESH
VROW, HOP, VCOL, PART, SUMS, DIRECT, ROWX, EXCH = range(8)

center_shift = 0.5
half_width = 3.0


def kernel(x_hbm, scale_hbm, places_hbm, count_hbm, blocks_hbm, out_ref, blk, tile, cur, prev, scale_ref, places, count,
           table_v, table, piece, hop, row0, row1, row2, row3, col0, col1, col2, col3, tsend, dsend, part, sums_send, sums, drecv, in_sem, send_sem, recv_sem,
           hop_sem, row_sem, col_sem, mate_sem, exch_sem, acc, exch, dsum):
    vrow, vcol = (row0, row1, row2, row3), (col0, col1, col2, col3)
    r = lax.axis_index("row")
    c = lax.axis_index("col")
    r_hi, r_lo = r // Q, lax.rem(r, Q)
    c_hi, c_lo = c // Q, lax.rem(c, Q)
    home_hi, home_lo = r_hi == c_hi, r_lo == c_lo
    half, core = c // 2, lax.rem(c, 2)
    mate = c + 1 - 2 * core
    relay_lo = lax.rem(r_lo + Q - 1 + 2 * core, Q)
    origin_lo = lax.rem(r_lo + Q + 1 - 2 * core, Q)

    loads = [
        pltpu.make_async_copy(src, dst, in_sem.at[i])
        for i, (src, dst) in enumerate(((x_hbm, cur), (scale_hbm, scale_ref), (places_hbm, places), (count_hbm, count),
                                        (blocks_hbm, blk.at[pl.ds(0, S)])))
    ]
    for load in loads:
        load.start()

    barrier = pltpu.get_barrier_semaphore()

    def signal(row, col):
        pl.semaphore_signal(barrier, inc=1, device_id=(row, col), device_id_type=MESH)

    def greet_row(k, _):
        signal(r, lax.rem(c + k, G))
        return 0

    lax.fori_loop(1, G, greet_row, 0)

    def greet_near(k, _):
        signal(r_hi * Q + lax.rem(r_lo + 1 + k // Q, Q), c_hi * Q + lax.rem(k, Q))
        return 0

    lax.fori_loop(0, Q * (Q - 1), greet_near, 0)
    for k in range(1, Q):
        signal(lax.rem(r_hi + k, Q) * Q + relay_lo, r_hi * Q + c_lo)
        signal(c_hi * Q + origin_lo, lax.rem(c_hi + k, Q) * Q + c_lo)
        signal(lax.rem(r_hi + k, Q) * Q + r_lo, r_hi * Q + c_lo)

    @pl.when(jnp.logical_not(home_hi))
    def _():
        signal(r_hi * Q + relay_lo, r_hi * Q + c_lo)
        signal(c_hi * Q + origin_lo, c_hi * Q + c_lo)
        for k in range(1, Q):
            signal(c_hi * Q + r_lo, lax.rem(r_hi + k, Q) * Q + c_lo)

    prev[...] = jnp.zeros((V, B), jnp.float32)
    blk[S] = jnp.zeros((B, B), jnp.bfloat16)

    loads[2].wait()
    loads[3].wait()
    lane = lax.broadcasted_iota(jnp.int32, (1, S), 1)
    at = jnp.where(lane < count[...], places[0:1, :] * G + places[1:2, :], -1)
    row_id = lax.broadcasted_iota(jnp.int32, (S, S), 0)
    col_id = lax.broadcasted_iota(jnp.int32, (S, S), 1)
    for upper in range(2):
        slot = jnp.min(jnp.where(row_id + upper * S == at, col_id, S), axis=1, keepdims=True)
        table_v[upper : upper + 1, :] = jnp.min(jnp.where(row_id == col_id, slot, S), axis=0, keepdims=True)
    to_scalars = pltpu.make_async_copy(table_v, table, in_sem.at[5])
    to_scalars.start()
    loads[0].wait()
    loads[1].wait()
    with jax.named_scope("load"):
        loads[4].wait()
        to_scalars.wait()

    def build(i, _):
        for j in range(G):
            slot = jnp.clip(table[i // 8, lax.rem(i, 8) * G + j], 0, S)
            tile[pl.ds(pl.multiple_of(i * B, B), B), pl.ds(j * B, B)] = blk[slot]
        return 0

    with jax.named_scope("build"):
        lax.fori_loop(0, G, build, 0)

    with jax.named_scope("barrier"):
        pl.semaphore_wait(barrier, G - 1 + Q * (Q - 1) + jnp.where(home_hi, 9, 14))

    def post(src, dst, kind, step, row, col, arrival=None):
        own = jnp.logical_and(row == r, col == c)
        arrival = recv_sem.at[kind, step] if arrival is None else arrival

        @pl.when(own)
        def _():
            pltpu.make_async_copy(src, dst, arrival).start()

        @pl.when(jnp.logical_not(own))
        def _():
            pltpu.make_async_remote_copy(src, dst, send_sem.at[kind, step], arrival, device_id=(row, col),
                                         device_id_type=MESH).start()

    def to_mate(src, dst, kind, step, arrival):
        pltpu.make_async_remote_copy(src, dst, send_sem.at[kind, step], arrival, device_id=(r, mate),
                                     device_id_type=MESH).start()

    def arrive(buf, kind, step):
        pltpu.make_async_copy(buf.at[step], buf.at[step], recv_sem.at[kind, step]).wait()

    def share(step):
        piece[step] = (scale_ref[...] * cur[...]).astype(jnp.bfloat16)

        for k in (2, 1, 3, 0):
            row, col = lax.rem(r_hi + k, Q) * Q + relay_lo, r_hi * Q + c_lo
            post(piece.at[step], hop.at[step, c_hi], HOP, step, row, col, hop_sem.at[step, c_hi])
        for k in (2, 1, 3, 0):
            hi = lax.rem(c_hi + k, Q)

            for i in range(2):
                post(piece.at[step], vrow[(Q - k) % Q].at[step, 2 * core + c_lo // 2], VROW, step, r, hi * Q + 2 * i + core,
                     row_sem.at[step, (Q - k) % Q])
        for k in (0, 1, 3, 2):
            pair = vrow[k].at[step, pl.ds(2 * core, 2)]
            pltpu.make_async_copy(pair, pair, row_sem.at[step, k]).wait()
            for i in range(2):
                both = vrow[k].at[step, 2 * core + i]
                to_mate(both, both, ROWX, step, mate_sem.at[step, k])
        for k in (0, 1, 3, 2):
            hi = lax.rem(c_hi + k, Q)
            pltpu.make_async_copy(hop.at[step, hi], hop.at[step, hi], hop_sem.at[step, hi]).wait()

            def spread(i, _):
                post(hop.at[step, hi], vcol[k].at[step, c_lo], VCOL, step, r_hi * Q + lax.rem(r_lo + i, Q), c_hi * Q + origin_lo,
                     col_sem.at[step, k])
                return 0

            lax.fori_loop(0, Q, spread, 0)

    def multiply(step, buf, sem, awaited, order, block, name, last, emit):
        for at, k in enumerate((0, 1, 3, 2)):
            hi = lax.rem(c_hi + k, Q)
            pieces = buf[k].at[step, awaited]
            with jax.named_scope("wait_" + name):
                pltpu.make_async_copy(pieces, pieces, sem.at[step, k]).wait()

            def term(n):
                v = jnp.concatenate([buf[k][step, u] for u in order], axis=1)
                total = block(v, pl.ds(pl.multiple_of(hi * Q * B, Q * B), Q * B), pl.ds(n * 2 * B, 2 * B))
                if at:
                    total += acc[n]
                if at < Q - 1:
                    acc[n] = total
                else:
                    last(n, total)

            with jax.named_scope("mm_" + name):
                for part_of in range(2):
                    for n in range(part_of * Q, part_of * Q + Q):
                        term(n)
                    if at == Q - 1:
                        emit(part_of)

    def transposed(step):
        def block(v, inner, outer):
            return jnp.dot(v, tile[inner, outer], preferred_element_type=jnp.float32)

        def last(n, total):
            for u in range(2):
                tsend[step, 2 * n + u] = total[:, u * B : (u + 1) * B].astype(jnp.bfloat16)

        def emit(part_of):
            def send(j, _):
                post(tsend.at[step, j], part.at[step, r_lo * Q + j // Q], PART, step, r_hi * Q + c_lo, c_hi * Q + lax.rem(j, Q))
                return 0

            lax.fori_loop(part_of * 2 * Q, part_of * 2 * Q + 2 * Q, send, 0)

        multiply(step, vrow, mate_sem, pl.ds(2 - 2 * core, 2), (0, 2, 1, 3), block, "row", last, emit)

    def meet(step):
        with jax.named_scope("wait_part"):
            arrive(part, PART, step)
        for k in range(Q):
            hi = lax.rem(c_hi + 2 + k, Q)
            total = jnp.zeros((V, B), jnp.float32)
            for lo in range(Q):
                total += part[step, lo * Q + hi].astype(jnp.float32)
            sums_send[step, k] = total.astype(jnp.bfloat16)
            post(sums_send.at[step, k], sums.at[step, r_hi], SUMS, step, c_hi * Q + r_lo, hi * Q + c_lo)

    def direct(step):
        def block(v, inner, outer):
            return lax.dot_general(v, tile[outer, inner], (((1,), (1,)), ((), ())), preferred_element_type=jnp.float32)

        def last(n, total):
            acc[n] = total
            dsend[step, n] = acc[n, :, pl.ds(pl.multiple_of((1 - core) * B, B), B)].astype(jnp.bfloat16)

        def emit(part_of):
            for n in range(part_of * Q, part_of * Q + Q):
                to_mate(dsend.at[step, n], exch.at[step, n], EXCH, step, exch_sem.at[step, part_of])

        multiply(step, vcol, col_sem, pl.ds(0, Q), range(Q), block, "col", last, emit)
        meet(step)
        for part_of in range(2):
            mine = exch.at[step, pl.ds(part_of * Q, Q)]
            with jax.named_scope("wait_mate"):
                pltpu.make_async_copy(mine, mine, exch_sem.at[step, part_of]).wait()
            for n in range(part_of * Q, part_of * Q + Q):
                own = acc[n, :, pl.ds(pl.multiple_of(core * B, B), B)]
                dsum[step, n] = (own + exch[step, n].astype(jnp.float32)).astype(jnp.bfloat16)

        def send(i, _):
            n = lax.rem(half + Q + i, G // 2)
            post(dsum.at[step, n], drecv.at[step, half], DIRECT, step, r, 2 * n + core)
            return 0

        lax.fori_loop(0, G // 2, send, 0)

    def collect(step):
        applied = jnp.zeros((V, B), jnp.float32)
        with jax.named_scope("wait_drecv"):
            arrive(drecv, DIRECT, step)
        for k in range(G // 2):
            applied += drecv[step, k].astype(jnp.float32)
        with jax.named_scope("wait_sums"):
            arrive(sums, SUMS, step)
        for k in range(Q):
            applied += sums[step, k].astype(jnp.float32)
        now = cur[...]
        mapped = scale_ref[...] * applied - center_shift * now
        factor = jnp.where(step == 0, 1.0 / half_width, 2.0 / half_width)
        updated = factor * mapped - prev[...]
        prev[...] = now
        cur[...] = updated

    def one_step(step, _):
        with jax.named_scope("share"):
            share(step)

        transposed(step)
        direct(step)
        collect(step)
        return 0

    lax.fori_loop(0, STEPS, one_step, 0)
    out_ref[...] = cur[...]

    def drain(step, _):
        def sent(kind, buf, n):
            done = buf.at[step, pl.ds(0, n)]
            pltpu.make_async_copy(done, done, send_sem.at[kind, step]).wait()

        for kind, n in ((VROW, G // 2 - 1), (DIRECT, G // 2 - 1), (ROWX, G // 2), (EXCH, G // 2)):
            sent(kind, part, n)
        sent(HOP, hop, Q)
        for kind, buf, n, home, own in ((SUMS, sums, Q, home_hi, 1), (VCOL, part, G, origin_lo == c_lo, Q),
                                        (PART, part, G, home_lo, Q)):
            sent(kind, buf, n - own)

            @pl.when(jnp.logical_not(home))
            def _():
                sent(kind, buf, own)

        return 0

    with jax.named_scope("drain"):
        lax.fori_loop(0, STEPS, drain, 0)


def per_device(start_vectors, scaling, block_values, block_places, block_counts):
    anywhere = pl.BlockSpec(memory_space=pl.ANY)

    def slab(n):
        return pltpu.VMEM((STEPS, n, V, B), jnp.bfloat16)

    f32 = pltpu.VMEM((V, B), jnp.float32)
    return pl.pallas_call(
        kernel,
        name="filter",
        out_shape=jax.ShapeDtypeStruct((V, B), jnp.float32),
        in_specs=[anywhere] * 5,
        out_specs=pl.BlockSpec(memory_space=pltpu.VMEM),
        scratch_shapes=[
            pltpu.VMEM((S + 1, B, B), jnp.bfloat16),
            pltpu.VMEM((G * B, G * B), jnp.bfloat16),
            f32,
            f32,
            pltpu.VMEM((1, B), jnp.float32),
            pltpu.VMEM((2, S), jnp.int32),
            pltpu.VMEM((1, 1), jnp.int32),
            pltpu.VMEM((2, S), jnp.int32),
            pltpu.SMEM((2, S), jnp.int32),
            pltpu.VMEM((STEPS, V, B), jnp.bfloat16),
            slab(Q), *[slab(Q)] * 8, slab(G), slab(G // 2), slab(G), slab(Q), slab(Q), slab(G // 2),
            pltpu.SemaphoreType.DMA((6,)),
            pltpu.SemaphoreType.DMA((8, STEPS)),
            pltpu.SemaphoreType.DMA((8, STEPS)),
            pltpu.SemaphoreType.DMA((STEPS, Q)),
            pltpu.SemaphoreType.DMA((STEPS, Q)),
            pltpu.SemaphoreType.DMA((STEPS, Q)),
            pltpu.SemaphoreType.DMA((STEPS, Q)),
            pltpu.SemaphoreType.DMA((STEPS, 2)),
            pltpu.VMEM((G // 2, V, 2 * B), jnp.float32),
            slab(G // 2), slab(G // 2),
        ],
        compiler_params=pltpu.CompilerParams(collective_id=0, has_side_effects=True, vmem_limit_bytes=60 << 20),
    )(start_vectors, scaling.reshape(1, B), block_places.reshape(2, S), block_counts, block_values.reshape(S, B, B))


def solution(mesh):
    in_specs = (
        P(None, ("row", "col")),
        P(("row", "col")),
        P("row", "col", None, None, None),
        P("row", "col", None, None),
        P("row", "col"),
    )
    out_specs = P(None, ("row", "col"))
    return jax.shard_map(
        per_device, mesh=mesh, in_specs=in_specs, out_specs=out_specs, check_vma=False
    )
```

time: 85.6 us -> 80.3 us (0.938)
  Pallas kernels: 82.2 us -> 77.6 us
    pallas_call x1, Pallas kernels: 82.2 us -> 77.6 us  [per_device(): pl.pallas_call(kernel, name='filter', out_shape=jax.ShapeDtypeStruct((V,...]
where the time goes in v4:
time: 80.3 us; the launch traced here: 79.6 us
  Pallas kernels  77.6 us (97%)
  local copies, waits for them, and re-layouts  1.38 us (2%)
    pallas_call x1, Pallas kernels, per_device(): pl.pallas_call(kernel, name='filter', out_shape=jax.ShapeDtypeStruct((V,...  77.6 us

profile of v4, /device:TPU:8, one launch (start us, length us, event | category | flops | bytes accessed | tf_op | source)
XLA Modules:
  0.0 79.6 jit_solution(14441446833299731857)
XLA Ops:
  0.7 77.6 %filter.1 = f32[64,128]{1,0:T(8,128)} custom-call(f32[64,128]{1,0:T(8,128)} %x_hbm.1, f32[1,128]{1,0:T(1,128)} %bitcast.5, s32[2,128]{1,0:T(2,128)} %bitcast.4, s32[1,1]{1,0:T(1,128)S(6)} %copy.7.count_hbm, bf16[128,128,128]{2,1,0:T(8,128)(2,1)} %bitcast.3), custom_call_target="tpu_custom_call" | custom-call | tf_op jit(solution)/shard_map/filter/pallas_call | solution.py:291
  78.2 1.4 %copy.8 = f32[64,128]{1,0:T(8,128)} copy(f32[64,128]{1,0:T(8,128)} %filter.1) | data formatting | bytes 65536

commit v5 on v4

--- a/solution.py
+++ b/solution.py
@@ -45,17 +45,6 @@
     def signal(row, col):
         pl.semaphore_signal(barrier, inc=1, device_id=(row, col), device_id_type=MESH)
 
-    def greet_row(k, _):
-        signal(r, lax.rem(c + k, G))
-        return 0
-
-    lax.fori_loop(1, G, greet_row, 0)
-
-    def greet_near(k, _):
-        signal(r_hi * Q + lax.rem(r_lo + 1 + k // Q, Q), c_hi * Q + lax.rem(k, Q))
-        return 0
-
-    lax.fori_loop(0, Q * (Q - 1), greet_near, 0)
     for k in range(1, Q):
         signal(lax.rem(r_hi + k, Q) * Q + relay_lo, r_hi * Q + c_lo)
         signal(c_hi * Q + origin_lo, lax.rem(c_hi + k, Q) * Q + c_lo)
@@ -68,6 +57,17 @@
         for k in range(1, Q):
             signal(c_hi * Q + r_lo, lax.rem(r_hi + k, Q) * Q + c_lo)
 
+    def greet_row(k, _):
+        signal(r, lax.rem(c + k, G))
+        return 0
+
+    lax.fori_loop(1, G, greet_row, 0)
+
+    def greet_near(k, _):
+        signal(r_hi * Q + lax.rem(r_lo + 1 + k // Q, Q), c_hi * Q + lax.rem(k, Q))
+        return 0
+
+    lax.fori_loop(0, Q * (Q - 1), greet_near, 0)
     prev[...] = jnp.zeros((V, B), jnp.float32)
     blk[S] = jnp.zeros((B, B), jnp.bfloat16)
 
@@ -84,25 +84,22 @@
     to_scalars.start()
     loads[0].wait()
     loads[1].wait()
-    with jax.named_scope("load"):
-        loads[4].wait()
-        to_scalars.wait()
-
     def build(i, _):
         for j in range(G):
             slot = jnp.clip(table[i // 8, lax.rem(i, 8) * G + j], 0, S)
             tile[pl.ds(pl.multiple_of(i * B, B), B), pl.ds(j * B, B)] = blk[slot]
         return 0
 
-    with jax.named_scope("build"):
-        lax.fori_loop(0, G, build, 0)
-
     with jax.named_scope("barrier"):
         pl.semaphore_wait(barrier, G - 1 + Q * (Q - 1) + jnp.where(home_hi, 9, 14))
 
-    def post(src, dst, kind, step, row, col, arrival=None):
-        own = jnp.logical_and(row == r, col == c)
-        arrival = recv_sem.at[kind, step] if arrival is None else arrival
+    def push(src, dst, kind, step, row, col, arrival):
+        pltpu.make_async_remote_copy(src, dst, send_sem.at[kind, step], arrival, device_id=(row, col), device_id_type=MESH).start()
+
+    def post(src, dst, kind, step, row, col, arrival, own):
+        if own is True:
+            pltpu.make_async_copy(src, dst, arrival).start()
+            return
 
         @pl.when(own)
         def _():
@@ -110,8 +107,7 @@
 
         @pl.when(jnp.logical_not(own))
         def _():
-            pltpu.make_async_remote_copy(src, dst, send_sem.at[kind, step], arrival, device_id=(row, col),
-                                         device_id_type=MESH).start()
+            push(src, dst, kind, step, row, col, arrival)
 
     def to_mate(src, dst, kind, step, arrival):
         pltpu.make_async_remote_copy(src, dst, send_sem.at[kind, step], arrival, device_id=(r, mate),
@@ -125,29 +121,37 @@
 
         for k in (2, 1, 3, 0):
             row, col = lax.rem(r_hi + k, Q) * Q + relay_lo, r_hi * Q + c_lo
-            post(piece.at[step], hop.at[step, c_hi], HOP, step, row, col, hop_sem.at[step, c_hi])
+            push(piece.at[step], hop.at[step, c_hi], HOP, step, row, col, hop_sem.at[step, c_hi])
         for k in (2, 1, 3, 0):
             hi = lax.rem(c_hi + k, Q)
 
             for i in range(2):
-                post(piece.at[step], vrow[(Q - k) % Q].at[step, 2 * core + c_lo // 2], VROW, step, r, hi * Q + 2 * i + core,
-                     row_sem.at[step, (Q - k) % Q])
+                there, arrival = vrow[(Q - k) % Q].at[step, 2 * core + c_lo // 2], row_sem.at[step, (Q - k) % Q]
+                col = hi * Q + 2 * lax.rem(c_lo // 2 + 1 - i, 2) + core
+                if k or not i:
+                    push(piece.at[step], there, VROW, step, r, col, arrival)
+                else:
+                    post(piece.at[step], there, VROW, step, r, col, arrival, True)
+
+    def hand_over(step):
         for k in (0, 1, 3, 2):
             pair = vrow[k].at[step, pl.ds(2 * core, 2)]
             pltpu.make_async_copy(pair, pair, row_sem.at[step, k]).wait()
             for i in range(2):
                 both = vrow[k].at[step, 2 * core + i]
                 to_mate(both, both, ROWX, step, mate_sem.at[step, k])
+
+    def relay(step):
         for k in (0, 1, 3, 2):
             hi = lax.rem(c_hi + k, Q)
             pltpu.make_async_copy(hop.at[step, hi], hop.at[step, hi], hop_sem.at[step, hi]).wait()
 
-            def spread(i, _):
-                post(hop.at[step, hi], vcol[k].at[step, c_lo], VCOL, step, r_hi * Q + lax.rem(r_lo + i, Q), c_hi * Q + origin_lo,
-                     col_sem.at[step, k])
-                return 0
-
-            lax.fori_loop(0, Q, spread, 0)
+            for i in (2, 1, 3, 0):
+                row, col = r_hi * Q + lax.rem(r_lo + i, Q), c_hi * Q + origin_lo
+                if i:
+                    push(hop.at[step, hi], vcol[k].at[step, c_lo], VCOL, step, row, col, col_sem.at[step, k])
+                else:
+                    post(hop.at[step, hi], vcol[k].at[step, c_lo], VCOL, step, row, col, col_sem.at[step, k], origin_lo == c_lo)
 
     def multiply(step, buf, sem, awaited, order, block, name, last, emit):
         for at, k in enumerate((0, 1, 3, 2)):
@@ -182,11 +186,15 @@
                 tsend[step, 2 * n + u] = total[:, u * B : (u + 1) * B].astype(jnp.bfloat16)
 
         def emit(part_of):
-            def send(j, _):
-                post(tsend.at[step, j], part.at[step, r_lo * Q + j // Q], PART, step, r_hi * Q + c_lo, c_hi * Q + lax.rem(j, Q))
-                return 0
-
-            lax.fori_loop(part_of * 2 * Q, part_of * 2 * Q + 2 * Q, send, 0)
+            for y in range(2 * part_of, 2 * part_of + 2):
+                for i in range(Q):
+                    lo = lax.rem(c_lo + i, Q)
+                    src, dst = tsend.at[step, y * Q + lo], part.at[step, r_lo * Q + y]
+                    row, col = r_hi * Q + c_lo, c_hi * Q + lo
+                    if i:
+                        push(src, dst, PART, step, row, col, recv_sem.at[PART, step])
+                    else:
+                        post(src, dst, PART, step, row, col, recv_sem.at[PART, step], home_lo)
 
         multiply(step, vrow, mate_sem, pl.ds(2 - 2 * core, 2), (0, 2, 1, 3), block, "row", last, emit)
 
@@ -199,7 +207,11 @@
             for lo in range(Q):
                 total += part[step, lo * Q + hi].astype(jnp.float32)
             sums_send[step, k] = total.astype(jnp.bfloat16)
-            post(sums_send.at[step, k], sums.at[step, r_hi], SUMS, step, c_hi * Q + r_lo, hi * Q + c_lo)
+            row, col, arrival = c_hi * Q + r_lo, hi * Q + c_lo, recv_sem.at[SUMS, step]
+            if k != 2:
+                push(sums_send.at[step, k], sums.at[step, r_hi], SUMS, step, row, col, arrival)
+            else:
+                post(sums_send.at[step, k], sums.at[step, r_hi], SUMS, step, row, col, arrival, home_hi)
 
     def direct(step):
         def block(v, inner, outer):
@@ -223,12 +235,13 @@
                 own = acc[n, :, pl.ds(pl.multiple_of(core * B, B), B)]
                 dsum[step, n] = (own + exch[step, n].astype(jnp.float32)).astype(jnp.bfloat16)
 
-        def send(i, _):
+        for i in range(G // 2):
             n = lax.rem(half + Q + i, G // 2)
-            post(dsum.at[step, n], drecv.at[step, half], DIRECT, step, r, 2 * n + core)
-            return 0
-
-        lax.fori_loop(0, G // 2, send, 0)
+            src, dst, arrival = dsum.at[step, n], drecv.at[step, half], recv_sem.at[DIRECT, step]
+            if i != Q:
+                push(src, dst, DIRECT, step, r, 2 * n + core, arrival)
+            else:
+                post(src, dst, DIRECT, step, r, 2 * n + core, arrival, True)
 
     def collect(step):
         applied = jnp.zeros((V, B), jnp.float32)
@@ -248,9 +261,19 @@
         cur[...] = updated
 
     def one_step(step, _):
-        with jax.named_scope("share"):
-            share(step)
-
+        share(step)
+
+        @pl.when(step == 0)
+        def _():
+            with jax.named_scope("build"):
+                loads[4].wait()
+                to_scalars.wait()
+                lax.fori_loop(0, G, build, 0)
+
+        with jax.named_scope("hand_over"):
+            hand_over(step)
+        with jax.named_scope("relay"):
+            relay(step)
         transposed(step)
         direct(step)
         collect(step)

time: 80.3 us -> 78.2 us (0.974)
  Pallas kernels: 77.6 us -> 76 us
    pallas_call x1, Pallas kernels: 77.6 us -> 76 us  [per_device(): pl.pallas_call(kernel, name='filter', out_shape=jax.ShapeDtypeStruct((V,...]
where the time goes in v5:
time: 78.2 us; the launch traced here: 78 us
  Pallas kernels  76 us (97%)
  local copies, waits for them, and re-layouts  1.38 us (2%)
    pallas_call x1, Pallas kernels, per_device(): pl.pallas_call(kernel, name='filter', out_shape=jax.ShapeDtypeStruct((V,...  76 us

profile of v5, /device:TPU:8, one launch (start us, length us, event | category | flops | bytes accessed | tf_op | source)
XLA Modules:
  0.0 78.0 jit_solution(3387746839494606232)
XLA Ops:
  0.7 76.0 %filter.1 = f32[64,128]{1,0:T(8,128)} custom-call(f32[64,128]{1,0:T(8,128)} %x_hbm.1, f32[1,128]{1,0:T(1,128)} %bitcast.5, s32[2,128]{1,0:T(2,128)} %bitcast.4, s32[1,1]{1,0:T(1,128)S(6)} %copy.7.count_hbm, bf16[128,128,128]{2,1,0:T(8,128)(2,1)} %bitcast.3), custom_call_target="tpu_custom_call" | custom-call | tf_op jit(solution)/shard_map/filter/pallas_call | solution.py:314
  76.7 1.4 %copy.8 = f32[64,128]{1,0:T(8,128)} copy(f32[64,128]{1,0:T(8,128)} %filter.1) | data formatting | bytes 65536

commit v6 on v5

--- a/solution.py
+++ b/solution.py
@@ -185,18 +185,31 @@
             for u in range(2):
                 tsend[step, 2 * n + u] = total[:, u * B : (u + 1) * B].astype(jnp.bfloat16)
 
-        def emit(part_of):
-            for y in range(2 * part_of, 2 * part_of + 2):
-                for i in range(Q):
-                    lo = lax.rem(c_lo + i, Q)
-                    src, dst = tsend.at[step, y * Q + lo], part.at[step, r_lo * Q + y]
-                    row, col = r_hi * Q + c_lo, c_hi * Q + lo
-                    if i:
-                        push(src, dst, PART, step, row, col, recv_sem.at[PART, step])
-                    else:
-                        post(src, dst, PART, step, row, col, recv_sem.at[PART, step], home_lo)
-
-        multiply(step, vrow, mate_sem, pl.ds(2 - 2 * core, 2), (0, 2, 1, 3), block, "row", last, emit)
+        def emit(y):
+            for i in range(Q):
+                lo = lax.rem(c_lo + i, Q)
+                src, dst = tsend.at[step, y * Q + lo], part.at[step, r_lo * Q + y]
+                row, col = r_hi * Q + c_lo, c_hi * Q + lo
+                if i:
+                    push(src, dst, PART, step, row, col, recv_sem.at[PART, step])
+                else:
+                    post(src, dst, PART, step, row, col, recv_sem.at[PART, step], home_lo)
+
+        with jax.named_scope("wait_row"):
+            for k in (0, 1, 3, 2):
+                pieces = vrow[k].at[step, pl.ds(2 - 2 * core, 2)]
+                pltpu.make_async_copy(pieces, pieces, mate_sem.at[step, k]).wait()
+        with jax.named_scope("mm_row"):
+            for y in range(0, Q, 1):
+                for n in range(2 * y, 2 * y + 2):
+                    total = jnp.zeros((V, 2 * B), jnp.float32)
+                    for k in range(Q):
+                        hi = lax.rem(c_hi + k, Q)
+                        v = jnp.concatenate([vrow[k][step, u] for u in (0, 2, 1, 3)], axis=1)
+                        total += block(v, pl.ds(pl.multiple_of(hi * Q * B, Q * B), Q * B), pl.ds(n * 2 * B, 2 * B))
+                    last(n, total)
+                for ready in range(y, y + 1):
+                    emit(ready)
 
     def meet(step):
         with jax.named_scope("wait_part"):

time: 78.2 us -> 77.5 us (level)
  no operation moved by 1% of the time
where the time goes in v6:
time: 77.5 us; the launch traced here: 77.3 us
  Pallas kernels  75.3 us (97%)
  local copies, waits for them, and re-layouts  1.38 us (2%)
    pallas_call x1, Pallas kernels, per_device(): pl.pallas_call(kernel, name='filter', out_shape=jax.ShapeDtypeStruct((V,...  75.3 us

profile of v6, /device:TPU:8, one launch (start us, length us, event | category | flops | bytes accessed | tf_op | source)
XLA Modules:
  0.0 77.3 jit_solution(12169708231733814743)
XLA Ops:
  0.7 75.3 %filter.1 = f32[64,128]{1,0:T(8,128)} custom-call(f32[64,128]{1,0:T(8,128)} %x_hbm.1, f32[1,128]{1,0:T(1,128)} %bitcast.5, s32[2,128]{1,0:T(2,128)} %bitcast.4, s32[1,1]{1,0:T(1,128)S(6)} %copy.7.count_hbm, bf16[128,128,128]{2,1,0:T(8,128)(2,1)} %bitcast.3), custom_call_target="tpu_custom_call" | custom-call | tf_op jit(solution)/shard_map/filter/pallas_call | solution.py:327
  75.9 1.4 %copy.8 = f32[64,128]{1,0:T(8,128)} copy(f32[64,128]{1,0:T(8,128)} %filter.1) | data formatting | bytes 65536

commit v7 on v6

--- a/solution.py
+++ b/solution.py
@@ -247,14 +247,8 @@
             for n in range(part_of * Q, part_of * Q + Q):
                 own = acc[n, :, pl.ds(pl.multiple_of(core * B, B), B)]
                 dsum[step, n] = (own + exch[step, n].astype(jnp.float32)).astype(jnp.bfloat16)
-
-        for i in range(G // 2):
-            n = lax.rem(half + Q + i, G // 2)
-            src, dst, arrival = dsum.at[step, n], drecv.at[step, half], recv_sem.at[DIRECT, step]
-            if i != Q:
-                push(src, dst, DIRECT, step, r, 2 * n + core, arrival)
-            else:
-                post(src, dst, DIRECT, step, r, 2 * n + core, arrival, True)
+            for n in range(part_of * Q, part_of * Q + Q):
+                post(dsum.at[step, n], drecv.at[step, half], DIRECT, step, r, 2 * n + core, recv_sem.at[DIRECT, step], half == n)
 
     def collect(step):
         applied = jnp.zeros((V, B), jnp.float32)

time: 77.5 us -> 77 us (level)
  no operation moved by 1% of the time
where the time goes in v7:
time: 77 us; the launch traced here: 76.9 us
  Pallas kernels  74.8 us (97%)
  local copies, waits for them, and re-layouts  1.38 us (2%)
    pallas_call x1, Pallas kernels, per_device(): pl.pallas_call(kernel, name='filter', out_shape=jax.ShapeDtypeStruct((V,...  74.8 us

profile of v7, /device:TPU:8, one launch (start us, length us, event | category | flops | bytes accessed | tf_op | source)
XLA Modules:
  0.0 76.9 jit_solution(6520018735737550263)
XLA Ops:
  0.7 74.8 %filter.1 = f32[64,128]{1,0:T(8,128)} custom-call(f32[64,128]{1,0:T(8,128)} %x_hbm.1, f32[1,128]{1,0:T(1,128)} %bitcast.5, s32[2,128]{1,0:T(2,128)} %bitcast.4, s32[1,1]{1,0:T(1,128)S(6)} %copy.7.count_hbm, bf16[128,128,128]{2,1,0:T(8,128)(2,1)} %bitcast.3), custom_call_target="tpu_custom_call" | custom-call | tf_op jit(solution)/shard_map/filter/pallas_call | solution.py:321
  75.5 1.4 %copy.8 = f32[64,128]{1,0:T(8,128)} copy(f32[64,128]{1,0:T(8,128)} %filter.1) | data formatting | bytes 65536

commit v8 on v7

--- a/solution.py
+++ b/solution.py
@@ -171,8 +171,8 @@
                     last(n, total)
 
             with jax.named_scope("mm_" + name):
-                for part_of in range(2):
-                    for n in range(part_of * Q, part_of * Q + Q):
+                for part_of in range(Q):
+                    for n in range(part_of * 2, part_of * 2 + 2):
                         term(n)
                     if at == Q - 1:
                         emit(part_of)
@@ -235,19 +235,19 @@
             dsend[step, n] = acc[n, :, pl.ds(pl.multiple_of((1 - core) * B, B), B)].astype(jnp.bfloat16)
 
         def emit(part_of):
-            for n in range(part_of * Q, part_of * Q + Q):
+            for n in range(part_of * 2, part_of * 2 + 2):
                 to_mate(dsend.at[step, n], exch.at[step, n], EXCH, step, exch_sem.at[step, part_of])
 
         multiply(step, vcol, col_sem, pl.ds(0, Q), range(Q), block, "col", last, emit)
         meet(step)
-        for part_of in range(2):
-            mine = exch.at[step, pl.ds(part_of * Q, Q)]
+        for part_of in range(Q):
+            mine = exch.at[step, pl.ds(part_of * 2, 2)]
             with jax.named_scope("wait_mate"):
                 pltpu.make_async_copy(mine, mine, exch_sem.at[step, part_of]).wait()
-            for n in range(part_of * Q, part_of * Q + Q):
+            for n in range(part_of * 2, part_of * 2 + 2):
                 own = acc[n, :, pl.ds(pl.multiple_of(core * B, B), B)]
                 dsum[step, n] = (own + exch[step, n].astype(jnp.float32)).astype(jnp.bfloat16)
-            for n in range(part_of * Q, part_of * Q + Q):
+            for n in range(part_of * 2, part_of * 2 + 2):
                 post(dsum.at[step, n], drecv.at[step, half], DIRECT, step, r, 2 * n + core, recv_sem.at[DIRECT, step], half == n)
 
     def collect(step):
@@ -343,7 +343,7 @@
             pltpu.SemaphoreType.DMA((STEPS, Q)),
             pltpu.SemaphoreType.DMA((STEPS, Q)),
             pltpu.SemaphoreType.DMA((STEPS, Q)),
-            pltpu.SemaphoreType.DMA((STEPS, 2)),
+            pltpu.SemaphoreType.DMA((STEPS, Q)),
             pltpu.VMEM((G // 2, V, 2 * B), jnp.float32),
             slab(G // 2), slab(G // 2),
         ],

time: 77 us -> 77.7 us (level)
  no operation moved by 1% of the time
where the time goes in v8:
time: 77.7 us; the launch traced here: 77.5 us
  Pallas kernels  75.5 us (97%)
  local copies, waits for them, and re-layouts  1.38 us (2%)
    pallas_call x1, Pallas kernels, per_device(): pl.pallas_call(kernel, name='filter', out_shape=jax.ShapeDtypeStruct((V,...  75.5 us

profile of v8, /device:TPU:8, one launch (start us, length us, event | category | flops | bytes accessed | tf_op | source)
XLA Modules:
  0.0 77.5 jit_solution(16235693928946873758)
XLA Ops:
  0.7 75.5 %filter.1 = f32[64,128]{1,0:T(8,128)} custom-call(f32[64,128]{1,0:T(8,128)} %x_hbm.1, f32[1,128]{1,0:T(1,128)} %bitcast.5, s32[2,128]{1,0:T(2,128)} %bitcast.4, s32[1,1]{1,0:T(1,128)S(6)} %copy.7.count_hbm, bf16[128,128,128]{2,1,0:T(8,128)(2,1)} %bitcast.3), custom_call_target="tpu_custom_call" | custom-call | tf_op jit(solution)/shard_map/filter/pallas_call | solution.py:321
  76.2 1.4 %copy.8 = f32[64,128]{1,0:T(8,128)} copy(f32[64,128]{1,0:T(8,128)} %filter.1) | data formatting | bytes 65536
